TPU v7x, 32 devices: a whole 2x2x4 slice. The times are simulated.
32 devices in a mesh: seq: 8 (over z, x), head: 4 (over y, core).
Axes of the slice: x: 2, y: 2, z: 4, core: 2. Of those that a mesh axis runs over, the one named last changes fastest.
Arguments:
- queries: bfloat16 [2048, 32, 128], P('seq', 'head'), may hold values from -6 to 6
- key_vectors: bfloat16 [2048, 4, 128], P(('seq', 'head')), may hold values from -6 to 6
- value_vectors: bfloat16 [2048, 4, 128], P(('seq', 'head')), may hold values from -6 to 6
- out_grad: bfloat16 [2048, 32, 128], P('seq', 'head'), may hold values from -6 to 6
Outputs:
- attended: bfloat16 [2048, 32, 128], P('seq', 'head')
- query_grad: bfloat16 [2048, 32, 128], P('seq', 'head')
- key_grad: bfloat16 [2048, 4, 128], P(('seq', 'head'))
- value_grad: bfloat16 [2048, 4, 128], P(('seq', 'head'))
All inputs are finite; a program needn't handle non-finite values.
Results may differ from a plain program's by a relative error of at most 0.035.
Values may be sent and summed in bfloat16 or wider, within the bound.
A program may use at most 64 MiB of HBM per device.

v0:
```python
import math

import jax
import jax.numpy as jnp
from jax import lax
from jax.sharding import PartitionSpec as P

GROUPS = 4


def shifted(value, axis, by):
    size = lax.axis_size(axis)
    return lax.ppermute(value, axis, [(i, (i + by) % size) for i in range(size)])


def visible(query_pos, key_pos, group_len, offset, tok_total):
    query_aligned = (query_pos - offset) % tok_total
    key_aligned = (key_pos - offset) % tok_total
    same_group = query_aligned[:, None] // group_len == key_aligned[None, :] // group_len
    return same_group & (key_aligned[None, :] <= query_aligned[:, None])


def per_device(queries, key_vectors, value_vectors, out_grad):
    key_home, value_home = (
        lax.all_to_all(key_vectors, "head", split_axis=1, concat_axis=0, tiled=True),
        lax.all_to_all(value_vectors, "head", split_axis=1, concat_axis=0, tiled=True),
    )
    key_home = key_home[:, 0, :]
    value_home = value_home[:, 0, :]
    tok_rows = queries.shape[0]
    half_heads = queries.shape[1] // 2
    head_dim = queries.shape[2]
    score_scale = 1.0 / math.sqrt(head_dim)
    devices = lax.axis_size("seq")
    group_span = devices // GROUPS
    tok_total = devices * tok_rows
    group_len = tok_total // GROUPS
    offsets = (0, group_len // 2)
    my_index = lax.axis_index("seq")
    local_pos = jnp.arange(tok_rows, dtype=jnp.int32)
    query_pos = my_index * tok_rows + local_pos
    q_parts = (queries[:, :half_heads], queries[:, half_heads:])
    grad_parts = (out_grad[:, :half_heads], out_grad[:, half_heads:])

    def key_positions(distance):
        return (my_index - distance) % devices * tok_rows + local_pos

    def scores_of(which_half, key_blk, allowed):
        scores = (
            jnp.einsum(
                "ihd,td->hit", q_parts[which_half], key_blk, preferred_element_type=jnp.float32
            )
            * score_scale
        )
        return jnp.where(allowed[None], scores, -jnp.inf)

    def forward_tile(states, key_blk, value_blk, distance):
        key_pos = key_positions(distance)
        updated = []
        for which_half in range(2):
            allowed = visible(query_pos, key_pos, group_len, offsets[which_half], tok_total)

            def forward_update(current, which_half=which_half, allowed=allowed):
                run_max, run_sum, running = current
                scores = scores_of(which_half, key_blk, allowed)
                new_max = jnp.maximum(run_max, jnp.max(scores, axis=2))
                weights = jnp.exp(scores - new_max[:, :, None])
                factor = jnp.exp(run_max - new_max)
                run_sum = run_sum * factor + jnp.sum(weights, axis=2)
                value_mix = jnp.einsum(
                    "hit,td->ihd",
                    weights.astype(jnp.bfloat16),
                    value_blk,
                    preferred_element_type=jnp.float32,
                )
                running = running * factor.T[:, :, None] + value_mix
                return (new_max, run_sum, running)

            updated.append(
                lax.cond(
                    jnp.any(allowed), forward_update, lambda current: current, states[which_half]
                )
            )
        return tuple(updated)

    def initial_state():
        return (
            jnp.full((half_heads, tok_rows), -jnp.inf, jnp.float32),
            jnp.zeros((half_heads, tok_rows), jnp.float32),
            jnp.zeros((tok_rows, half_heads, head_dim), jnp.float32),
        )

    forward_init = (initial_state(), initial_state())
    levels = (group_span - 1).bit_length()
    window_keys = key_home[None]
    window_values = value_home[None]
    for level_idx in range(levels):
        far_keys, far_values = shifted((window_keys, window_values), "seq", 2**level_idx)
        window_keys = jnp.concatenate([window_keys, far_keys], axis=0)
        window_values = jnp.concatenate([window_values, far_values], axis=0)

    def window_forward(distance, states):
        return forward_tile(states, window_keys[distance], window_values[distance], distance)

    states = lax.fori_loop(0, group_span, window_forward, forward_init)
    attended_parts = []
    log_totals = []
    deltas = []
    for which_half in range(2):
        run_max, run_sum, running = states[which_half]
        part_out = (running / run_sum.T[:, :, None]).astype(jnp.bfloat16)
        attended_parts.append(part_out)
        log_totals.append(run_max + jnp.log(run_sum))
        deltas.append(
            jnp.einsum(
                "ihd,ihd->hi", grad_parts[which_half], part_out, preferred_element_type=jnp.float32
            )
        )

    def backward_tile(current, key_blk, value_blk, distance):
        query_grads, key_acc, value_acc = current
        key_pos = key_positions(distance)
        new_query = []
        for which_half in range(2):
            allowed = visible(query_pos, key_pos, group_len, offsets[which_half], tok_total)

            def backward_update(inputs, which_half=which_half, allowed=allowed):
                query_acc, key_sum, value_sum = inputs
                scores = scores_of(which_half, key_blk, allowed)
                prob_full = jnp.exp(scores - log_totals[which_half][:, :, None])
                weights = prob_full.astype(jnp.bfloat16)
                prob_grad = jnp.einsum(
                    "ihd,td->hit",
                    grad_parts[which_half],
                    value_blk,
                    preferred_element_type=jnp.float32,
                )
                score_grad = (prob_full * (prob_grad - deltas[which_half][:, :, None])).astype(
                    jnp.bfloat16
                )
                query_acc = query_acc + jnp.einsum(
                    "hit,td->ihd", score_grad, key_blk, preferred_element_type=jnp.float32
                )
                key_sum = key_sum + jnp.einsum(
                    "hit,ihd->td",
                    score_grad,
                    q_parts[which_half],
                    preferred_element_type=jnp.float32,
                )
                value_sum = value_sum + jnp.einsum(
                    "hit,ihd->td",
                    weights,
                    grad_parts[which_half],
                    preferred_element_type=jnp.float32,
                )
                return (query_acc, key_sum, value_sum)

            query_acc, key_acc, value_acc = lax.cond(
                jnp.any(allowed),
                backward_update,
                lambda inputs: inputs,
                (query_grads[which_half], key_acc, value_acc),
            )
            new_query.append(query_acc)
        return (tuple(new_query), key_acc, value_acc)

    zero_query = jnp.zeros((tok_rows, half_heads, head_dim), jnp.float32)
    window_len = 2**levels
    key_buffer = jnp.zeros((window_len, tok_rows, head_dim), jnp.float32)
    value_buffer = jnp.zeros((window_len, tok_rows, head_dim), jnp.float32)

    def window_backward(distance, packed):
        query_grads, key_buffer, value_buffer = packed
        query_grads, key_acc, value_acc = backward_tile(
            (query_grads, key_buffer[distance], value_buffer[distance]),
            window_keys[distance],
            window_values[distance],
            distance,
        )
        key_buffer = lax.dynamic_update_index_in_dim(key_buffer, key_acc, distance, 0)
        value_buffer = lax.dynamic_update_index_in_dim(value_buffer, value_acc, distance, 0)
        return (query_grads, key_buffer, value_buffer)

    query_grads, key_buffer, value_buffer = lax.fori_loop(
        0, group_span, window_backward, ((zero_query, zero_query), key_buffer, value_buffer)
    )
    for level_idx in reversed(range(levels)):
        reach_len = 2**level_idx
        far_keys, far_values = (
            shifted(
                key_buffer[reach_len : 2 * reach_len].astype(jnp.bfloat16), "seq", -reach_len
            ).astype(jnp.float32),
            shifted(
                value_buffer[reach_len : 2 * reach_len].astype(jnp.bfloat16), "seq", -reach_len
            ).astype(jnp.float32),
        )
        key_buffer = key_buffer[:reach_len] + far_keys
        value_buffer = value_buffer[:reach_len] + far_values
    key_acc = key_buffer[0]
    value_acc = value_buffer[0]
    attended = jnp.concatenate(attended_parts, axis=1)
    query_grad = (jnp.concatenate(query_grads, axis=1) * score_scale).astype(jnp.bfloat16)
    key_home_grad = (key_acc * score_scale).astype(jnp.bfloat16)[:, None, :]
    value_home_grad = value_acc.astype(jnp.bfloat16)[:, None, :]
    key_grad, value_grad = (
        lax.all_to_all(key_home_grad, "head", split_axis=0, concat_axis=1, tiled=True),
        lax.all_to_all(value_home_grad, "head", split_axis=0, concat_axis=1, tiled=True),
    )
    return (attended, query_grad, key_grad, value_grad)


def solution(mesh):
    return jax.shard_map(
        per_device,
        mesh=mesh,
        in_specs=(
            P("seq", "head", None),
            P(("seq", "head"), None, None),
            P(("seq", "head"), None, None),
            P("seq", "head", None),
        ),
        out_specs=(
            P("seq", "head", None),
            P("seq", "head", None),
            P(("seq", "head"), None, None),
            P(("seq", "head"), None, None),
        ),
        check_vma=False,
    )
```

profile of v0, /device:TPU:0, one launch (start us, length us, event | category | flops | bytes accessed | tf_op | source)
XLA Modules:
  0.0 72.1 jit_solution(17380361485812917912)
XLA Ops:
  0.6 1.5 %copy.65 = bf16[64,4,128]{2,0,1:T(8,128)(2,1)} copy(bf16[64,4,128]{2,1,0:T(4,128)(2,1)} %param.18) | data formatting | bytes 131072 | tf_op args[2]
  2.1 4.3 %all-to-all-start.1 = ((bf16[64,4,128]{2,0,1:T(8,128)(2,1)}), bf16[64,4,128]{2,0,1:T(8,128)(2,1)S(1)}, u32[]{:S(2)}, u32[]{:S(2)}) async-start(bf16[64,4,128]{2,0,1:T(8,128)(2,1)} %copy.65), calls=%async_computation.1 | async-start | bytes 131072 | tf_op jit(solution)/shard_map/all_to_all | solution.py:26
  6.4 1.5 %fusion.88 = (bf16[256,4,128]{2,1,0:T(4,128)(2,1)S(1)}, bf16[256,4,128]{2,1,0:T(4,128)(2,1)S(1)}) fusion(bf16[256,8,128]{2,1,0:T(8,128)(2,1)} %param.16), kind=kLoop, calls=%fused_computation.186 | loop fusion | bytes 1048576 | tf_op jit(solution)/shard_map/slice | solution.py:42
  8.6 1.9 %all-to-all-done.1 = bf16[64,4,128]{2,0,1:T(8,128)(2,1)S(1)} async-done(((bf16[64,4,128]{2,0,1:T(8,128)(2,1)}), bf16[64,4,128]{2,0,1:T(8,128)(2,1)S(1)}, u32[]{:S(2)}, u32[]{:S(2)}) %all-to-all-start.1) | async-done | bytes 65568 | tf_op jit(solution)/shard_map/all_to_all | solution.py:26
  10.5 3.3 %all-to-all-start = ((bf16[64,4,128]{2,0,1:T(8,128)(2,1)}), bf16[64,4,128]{2,0,1:T(8,128)(2,1)S(1)}, u32[]{:S(2)}, u32[]{:S(2)}) async-start(bf16[64,4,128]{2,0,1:T(8,128)(2,1)} %copy.64), calls=%async_computation | async-start | bytes 131072 | tf_op jit(solution)/shard_map/all_to_all | solution.py:25
  13.8 2.0 %collective-permute-start.1 = (bf16[1,256,128]{2,1,0:T(8,128)(2,1)S(1)}, bf16[1,256,128]{2,1,0:T(8,128)(2,1)S(1)}, u32[]{:S(2)}, u32[]{:S(2)}) collective-permute-start(bf16[1,256,128]{2,1,0:T(8,128)(2,1)S(1)} %bitcast.190), channel_id=1, source_target_pairs={{0,4},{4,8},{8,12},{12,16},{16,20},{20,24},{24,28},{28,0},{1,5},{5... | collective-permute-start | bytes 196616 | tf_op jit(solution)/shard_map/ppermute | solution.py:13
  16.2 1.7 %all-to-all-done = bf16[64,4,128]{2,0,1:T(8,128)(2,1)S(1)} async-done(((bf16[64,4,128]{2,0,1:T(8,128)(2,1)}), bf16[64,4,128]{2,0,1:T(8,128)(2,1)S(1)}, u32[]{:S(2)}, u32[]{:S(2)}) %all-to-all-start) | async-done | bytes 65568 | tf_op jit(solution)/shard_map/all_to_all | solution.py:25
  17.9 2.0 %collective-permute-start = (bf16[1,256,128]{2,1,0:T(8,128)(2,1)S(1)}, bf16[1,256,128]{2,1,0:T(8,128)(2,1)S(1)}, u32[]{:S(2)}, u32[]{:S(2)}) collective-permute-start(bf16[1,256,128]{2,1,0:T(8,128)(2,1)S(1)} %bitcast.192), channel_id=1, source_target_pairs={{0,4},{4,8},{8,12},{12,16},{16,20},{20,24},{24,28},{28,0},{1,5},{5... | collective-permute-start | bytes 196616 | tf_op jit(solution)/shard_map/ppermute | solution.py:13
  19.8 1.7 %collective-permute-done.1 = bf16[1,256,128]{2,1,0:T(8,128)(2,1)S(1)} collective-permute-done((bf16[1,256,128]{2,1,0:T(8,128)(2,1)S(1)}, bf16[1,256,128]{2,1,0:T(8,128)(2,1)S(1)}, u32[]{:S(2)}, u32[]{:S(2)}) %collective-permute-start.1) | collective-permute-done | bytes 65568 | tf_op jit(solution)/shard_map/ppermute | solution.py:13
  21.5 3.6 %collective-permute-done = bf16[1,256,128]{2,1,0:T(8,128)(2,1)S(1)} collective-permute-done((bf16[1,256,128]{2,1,0:T(8,128)(2,1)S(1)}, bf16[1,256,128]{2,1,0:T(8,128)(2,1)S(1)}, u32[]{:S(2)}, u32[]{:S(2)}) %collective-permute-start) | collective-permute-done | bytes 65568 | tf_op jit(solution)/shard_map/ppermute | solution.py:13
  25.3 9.2 %while.54 = (s32[]{:T(128)}, f32[4,256]{1,0:T(4,128)S(1)}, f32[4,256]{1,0:T(4,128)S(1)}, f32[256,4,128]{2,0,1:T(8,128)S(1)}, f32[4,256]{1,0:T(4,128)S(1)}, /*ind...) while((s32[]{:T(128)}, f32[4,256]{1,0:T(4,128)S(1)}, ...), condition=%wide.region_11.12_spmd.clone.clone, body=%wide.region_0.11_spmd.clone.clone.sunk | while | flops 273188352 | bytes 9847346 | solution.py:105
  25.4 0.8 %fusion.107 = (pred[]{:T(512)}, pred[256,256]{0,1:T(8,128)(4,1)S(1)}) fusion(s32[256]{0:T(256)S(1)} %get-tuple-element.1754, s32[256]{0:T(256)S(1)} %get-tuple-element.1755, s32[256]{0:T(256)S(1)} %get-tuple-element.1756, s32[256]{0:T(256)S(1)} %get-tuple-element.1757), kind=kLoop, calls=%fused_computation.180.clone.1 | loop fusion | flops 262143 | bytes 69633 | tf_op jit(solution)/shard_map/while/body/eval_jaxpr/reduce_or | solution.py:81
  26.8 0.8 %fusion.108 = (pred[]{:T(512)}, pred[256,256]{0,1:T(8,128)(4,1)S(1)}) fusion(s32[256]{0:T(256)S(1)} %get-tuple-element.1765, s32[256]{0:T(256)S(1)} %get-tuple-element.1766, s32[256]{0:T(256)S(1)} %get-tuple-element.1767, s32[256]{0:T(256)S(1)} %get-tuple-element.1768), kind=kLoop, calls=%fused_computation.179.clone.1 | loop fusion | flops 262143 | bytes 69633 | tf_op jit(solution)/shard_map/while/body/eval_jaxpr/reduce_or | solution.py:81
  28.3 1.1 %conditional.16 = ((f32[4,256]{1,0:T(4,128)S(1)}, f32[4,256]{1,0:T(4,128)S(1)}, f32[256,4,128]{2,0,1:T(8,128)S(1)})) conditional(s32[]{:T(128)} %convert_element_type.157, (f32[4,256]{1,0:T(4,128)S(1)}, f32[4,256]{1,0:T(4,128)S(1)}, f32[256,4,128]{2,0,1:T(8,128)S(1)}) %tuple.217, (pred[256,256]{0,1:T(8,128)(4,1)S(1)}, bf16[256,128]{1,0:T(8,128)(2,1)S(1)}, ...), branch_computations={%region_2.2_spmd, %region_3.5_spmd} | conditional | flops 136317952 | bytes 4718624 | solution.py:80
  29.3 1.1 %conditional.17 = ((f32[4,256]{1,0:T(4,128)S(1)}, f32[4,256]{1,0:T(4,128)S(1)}, f32[256,4,128]{2,0,1:T(8,128)S(1)})) conditional(s32[]{:T(128)} %convert_element_type.158, (f32[4,256]{1,0:T(4,128)S(1)}, f32[4,256]{1,0:T(4,128)S(1)}, f32[256,4,128]{2,0,1:T(8,128)S(1)}) %tuple.219, (pred[256,256]{0,1:T(8,128)(4,1)S(1)}, ...), branch_computations={%region_7.7_spmd, %region_8.10_spmd} | conditional | flops 136317952 | bytes 4718624 | solution.py:80
  30.5 0.8 %fusion.107 = (pred[]{:T(512)}, pred[256,256]{0,1:T(8,128)(4,1)S(1)}) fusion(s32[256]{0:T(256)S(1)} %get-tuple-element.1754, s32[256]{0:T(256)S(1)} %get-tuple-element.1755, s32[256]{0:T(256)S(1)} %get-tuple-element.1756, s32[256]{0:T(256)S(1)} %get-tuple-element.1757), kind=kLoop, calls=%fused_computation.180.clone.1 | loop fusion | flops 262143 | bytes 69633 | tf_op jit(solution)/shard_map/while/body/eval_jaxpr/reduce_or | solution.py:81
  31.9 0.8 %fusion.108 = (pred[]{:T(512)}, pred[256,256]{0,1:T(8,128)(4,1)S(1)}) fusion(s32[256]{0:T(256)S(1)} %get-tuple-element.1765, s32[256]{0:T(256)S(1)} %get-tuple-element.1766, s32[256]{0:T(256)S(1)} %get-tuple-element.1767, s32[256]{0:T(256)S(1)} %get-tuple-element.1768), kind=kLoop, calls=%fused_computation.179.clone.1 | loop fusion | flops 262143 | bytes 69633 | tf_op jit(solution)/shard_map/while/body/eval_jaxpr/reduce_or | solution.py:81
  33.4 1.1 %conditional.17 = ((f32[4,256]{1,0:T(4,128)S(1)}, f32[4,256]{1,0:T(4,128)S(1)}, f32[256,4,128]{2,0,1:T(8,128)S(1)})) conditional(s32[]{:T(128)} %convert_element_type.158, (f32[4,256]{1,0:T(4,128)S(1)}, f32[4,256]{1,0:T(4,128)S(1)}, f32[256,4,128]{2,0,1:T(8,128)S(1)}) %tuple.219, (pred[256,256]{0,1:T(8,128)(4,1)S(1)}, ...), branch_computations={%region_7.7_spmd, %region_8.10_spmd} | conditional | flops 136317952 | bytes 4718624 | solution.py:80
  34.8 2.1 %bitcast_convert_fusion = (f32[4,256,128]{2,0,1:T(4,128)S(1)}, bf16[256,4,128]{2,1,0:T(4,128)(2,1)}, f32[4,256,128]{2,0,1:T(4,128)S(1)}, bf16[256,4,128]{2,1,0:T(4,128)(2,1)}) fusion(f32[256,4]{1,0:T(8,128)S(1)} %copy.70, f32[256,4,128]{2,0,1:T(8,128)S(1)} %get-tuple-element.1240, f32[256,4]{1,0:T(8,128)S(1)} %copy.68, ...), kind=kLoop, calls=%fused_computation.167 | loop fusion | flops 786432 | bytes 2629632
  37.5 11.2 %while.55 = (s32[]{:T(128)}, f32[256,4,128]{2,0,1:T(8,128)S(1)}, f32[256,4,128]{2,0,1:T(8,128)S(1)}, f32[2,256,128]{2,1,0:T(8,128)S(1)}, f32[2,256,128]{2,1,0:T(...) while((s32[]{:T(128)}, f32[256,4,128]{2,0,1:T(8,128)S(1)}, ...), condition=%wide.region_19.20_spmd.clone.clone, body=%wide.region_12.19_spmd.clone.clone.sunk | while | flops 675704320 | bytes 16679558 | solution.py:184
  37.6 0.8 %fusion.109 = (pred[]{:T(512)}, pred[256,256]{0,1:T(8,128)(4,1)S(1)}) fusion(s32[256]{0:T(256)S(1)} %get-tuple-element.1791, s32[256]{0:T(256)S(1)} %get-tuple-element.1792, s32[256]{0:T(256)S(1)} %get-tuple-element.1793, s32[256]{0:T(256)S(1)} %get-tuple-element.1794), kind=kLoop, calls=%fused_computation.182.clone.1 | loop fusion | flops 262143 | bytes 69633 | tf_op jit(solution)/shard_map/while/body/eval_jaxpr/reduce_or | solution.py:159
  40.5 1.7 %conditional.18 = ((f32[256,4,128]{2,0,1:T(8,128)S(1)}, f32[256,128]{1,0:T(8,128)S(1)}, f32[256,128]{1,0:T(8,128)S(1)})) conditional(s32[]{:T(128)} %convert_element_type.159, (f32[256,4,128]{2,0,1:T(8,128)S(1)}, f32[256,128]{1,0:T(8,128)S(1)}, f32[256,128]{1,0:T(8,128)S(1)}) %tuple.230, (pred[256,256]{0,1:T(8,128)(4,1)S(1)}, ...), branch_computations={%region_14.14_spmd, %region_15.15_spmd} | conditional | flops 337575936 | bytes 7610400 | solution.py:158
  42.2 1.7 %conditional.19 = (f32[256,4,128]{2,0,1:T(8,128)S(1)}, f32[1,256,128]{2,1,0:T(8,128)S(1)}, f32[1,256,128]{2,1,0:T(8,128)S(1)}) conditional(s32[]{:T(128)} %convert_element_type.160, (f32[256,4,128]{2,0,1:T(8,128)S(1)}, f32[256,128]{1,0:T(8,128)S(1)}, f32[256,128]{1,0:T(8,128)S(1)}) %tuple.248, (pred[256,256]{0,1:T(8,128)(4,1)S(1)}, ...), branch_computations={%region_17.17_spmd, %region_18.18_spmd} | conditional | flops 337575936 | bytes 7610392 | solution.py:158
  47.0 1.7 %conditional.19 = (f32[256,4,128]{2,0,1:T(8,128)S(1)}, f32[1,256,128]{2,1,0:T(8,128)S(1)}, f32[1,256,128]{2,1,0:T(8,128)S(1)}) conditional(s32[]{:T(128)} %convert_element_type.160, (f32[256,4,128]{2,0,1:T(8,128)S(1)}, f32[256,128]{1,0:T(8,128)S(1)}, f32[256,128]{1,0:T(8,128)S(1)}) %tuple.248, (pred[256,256]{0,1:T(8,128)(4,1)S(1)}, ...), branch_computations={%region_17.17_spmd, %region_18.18_spmd} | conditional | flops 337575936 | bytes 7610392 | solution.py:158
  49.1 2.1 %collective-permute-start.2 = (bf16[1,256,128]{2,1,0:T(8,128)(2,1)S(1)}, bf16[1,256,128]{2,1,0:T(8,128)(2,1)S(1)}, u32[]{:S(2)}, u32[]{:S(2)}) collective-permute-start(bf16[1,256,128]{2,1,0:T(8,128)(2,1)S(1)} %slice.45), channel_id=1, source_target_pairs={{0,28},{4,0},{8,4},{12,8},{16,12},{20,16},{24,20},{28,24},{1,29},{... | collective-permute-start | bytes 196616 | tf_op jit(solution)/shard_map/ppermute | solution.py:13
  51.1 1.4 %collective-permute-start.3 = (bf16[1,256,128]{2,1,0:T(8,128)(2,1)S(1)}, bf16[1,256,128]{2,1,0:T(8,128)(2,1)S(1)}, u32[]{:S(2)}, u32[]{:S(2)}) collective-permute-start(bf16[1,256,128]{2,1,0:T(8,128)(2,1)S(1)} %slice.44), channel_id=1, source_target_pairs={{0,28},{4,0},{8,4},{12,8},{16,12},{20,16},{24,20},{28,24},{1,29},{... | collective-permute-start | bytes 196616 | tf_op jit(solution)/shard_map/ppermute | solution.py:13
  53.6 1.1 %pad_maximum_fusion = bf16[256,8,128]{2,1,0:T(8,128)(2,1)} fusion(bf16[256,4,128]{2,1,0:T(4,128)(2,1)S(1)} %copy-done, bf16[256,4,128]{2,1,0:T(4,128)(2,1)S(1)} %copy-done.1), kind=kLoop, calls=%fused_computation.160 | loop fusion | flops 1048576 | bytes 1048576 | tf_op jit(solution)/shard_map/concatenate | solution.py:201
  56.5 3.3 %all-to-all-start.2 = ((bf16[4,2,4096]{2,1,0:T(2,128)(2,1)}), bf16[4,2,4096]{2,1,0:T(2,128)(2,1)S(1)}, u32[]{:S(2)}, u32[]{:S(2)}) async-start(bf16[4,2,4096]{2,1,0:T(2,128)(2,1)} %reshape.467), calls=%async_computation.2 | async-start | bytes 131072 | tf_op jit(solution)/shard_map/all_to_all | solution.py:206
  61.2 2.7 %all-to-all-done.2 = bf16[4,2,4096]{2,1,0:T(2,128)(2,1)S(1)} async-done(((bf16[4,2,4096]{2,1,0:T(2,128)(2,1)}), bf16[4,2,4096]{2,1,0:T(2,128)(2,1)S(1)}, u32[]{:S(2)}, u32[]{:S(2)}) %all-to-all-start.2) | async-done | bytes 65568 | tf_op jit(solution)/shard_map/all_to_all | solution.py:206
  63.9 3.3 %all-to-all-start.3 = ((bf16[4,2,4096]{2,1,0:T(2,128)(2,1)}), bf16[4,2,4096]{2,1,0:T(2,128)(2,1)S(1)}, u32[]{:S(2)}, u32[]{:S(2)}) async-start(bf16[4,2,4096]{2,1,0:T(2,128)(2,1)} %reshape.469), calls=%async_computation.3 | async-start | bytes 131072 | tf_op jit(solution)/shard_map/all_to_all | solution.py:207
  67.2 1.1 %fusion.74 = bf16[256,8,128]{2,1,0:T(8,128)(2,1)} fusion(f32[256,4,128]{2,1,0:T(4,128)S(1)} %copy.75, f32[256,4,128]{2,1,0:T(4,128)S(1)} %copy.74), kind=kLoop, calls=%fused_computation.159 | loop fusion | flops 786432 | bytes 1572864 | tf_op jit(solution)/shard_map/convert_element_type | solution.py:202
  69.0 2.2 %all-to-all-done.3 = bf16[4,2,4096]{2,1,0:T(2,128)(2,1)S(1)} async-done(((bf16[4,2,4096]{2,1,0:T(2,128)(2,1)}), bf16[4,2,4096]{2,1,0:T(2,128)(2,1)S(1)}, u32[]{:S(2)}, u32[]{:S(2)}) %all-to-all-start.3) | async-done | bytes 65568 | tf_op jit(solution)/shard_map/all_to_all | solution.py:207
  (114 shorter events, 18.7 us)
Async XLA Ops:
  2.1 8.4 %all-to-all-start.1 = ((bf16[64,4,128]{2,0,1:T(8,128)(2,1)}), bf16[64,4,128]{2,0,1:T(8,128)(2,1)S(1)}, u32[]{:S(2)}, u32[]{:S(2)}) async-start(bf16[64,4,128]{2,0,1:T(8,128)(2,1)} %copy.65), calls=%async_computation.1 | async-start | bytes 131072 | tf_op jit(solution)/shard_map/all_to_all | solution.py:26
  6.4 1.5 %copy-start.3 = (bf16[64,4,128]{2,1,0:T(4,128)(2,1)S(1)}, bf16[64,4,128]{2,1,0:T(4,128)(2,1)}, u32[]{:S(2)}) copy-start(bf16[64,4,128]{2,1,0:T(4,128)(2,1)} %param.17) | copy-start | bytes 196612
  6.4 9.4 %copy-start.2 = (bf16[256,8,128]{2,1,0:T(8,128)(2,1)S(1)}, bf16[256,8,128]{2,1,0:T(8,128)(2,1)}, u32[]{:S(2)}) copy-start(bf16[256,8,128]{2,1,0:T(8,128)(2,1)} %param.19) | copy-start | bytes 1572868
  10.5 7.4 %all-to-all-start = ((bf16[64,4,128]{2,0,1:T(8,128)(2,1)}), bf16[64,4,128]{2,0,1:T(8,128)(2,1)S(1)}, u32[]{:S(2)}, u32[]{:S(2)}) async-start(bf16[64,4,128]{2,0,1:T(8,128)(2,1)} %copy.64), calls=%async_computation | async-start | bytes 131072 | tf_op jit(solution)/shard_map/all_to_all | solution.py:25
  13.8 7.7 %collective-permute-start.1 = (bf16[1,256,128]{2,1,0:T(8,128)(2,1)S(1)}, bf16[1,256,128]{2,1,0:T(8,128)(2,1)S(1)}, u32[]{:S(2)}, u32[]{:S(2)}) collective-permute-start(bf16[1,256,128]{2,1,0:T(8,128)(2,1)S(1)} %bitcast.190), channel_id=1, source_target_pairs={{0,4},{4,8},{8,12},{12,16},{16,20},{20,24},{24,28},{28,0},{1,5},{5... | collective-permute-start | bytes 196616 | tf_op jit(solution)/shard_map/ppermute | solution.py:13
  17.9 7.2 %collective-permute-start = (bf16[1,256,128]{2,1,0:T(8,128)(2,1)S(1)}, bf16[1,256,128]{2,1,0:T(8,128)(2,1)S(1)}, u32[]{:S(2)}, u32[]{:S(2)}) collective-permute-start(bf16[1,256,128]{2,1,0:T(8,128)(2,1)S(1)} %bitcast.192), channel_id=1, source_target_pairs={{0,4},{4,8},{8,12},{12,16},{16,20},{20,24},{24,28},{28,0},{1,5},{5... | collective-permute-start | bytes 196616 | tf_op jit(solution)/shard_map/ppermute | solution.py:13
  49.1 5.6 %collective-permute-start.2 = (bf16[1,256,128]{2,1,0:T(8,128)(2,1)S(1)}, bf16[1,256,128]{2,1,0:T(8,128)(2,1)S(1)}, u32[]{:S(2)}, u32[]{:S(2)}) collective-permute-start(bf16[1,256,128]{2,1,0:T(8,128)(2,1)S(1)} %slice.45), channel_id=1, source_target_pairs={{0,28},{4,0},{8,4},{12,8},{16,12},{20,16},{24,20},{28,24},{1,29},{... | collective-permute-start | bytes 196616 | tf_op jit(solution)/shard_map/ppermute | solution.py:13
  51.1 8.7 %collective-permute-start.3 = (bf16[1,256,128]{2,1,0:T(8,128)(2,1)S(1)}, bf16[1,256,128]{2,1,0:T(8,128)(2,1)S(1)}, u32[]{:S(2)}, u32[]{:S(2)}) collective-permute-start(bf16[1,256,128]{2,1,0:T(8,128)(2,1)S(1)} %slice.44), channel_id=1, source_target_pairs={{0,28},{4,0},{8,4},{12,8},{16,12},{20,16},{24,20},{28,24},{1,29},{... | collective-permute-start | bytes 196616 | tf_op jit(solution)/shard_map/ppermute | solution.py:13
  52.6 0.9 %copy-start = (bf16[256,4,128]{2,1,0:T(4,128)(2,1)S(1)}, bf16[256,4,128]{2,1,0:T(4,128)(2,1)}, u32[]{:S(2)}) copy-start(bf16[256,4,128]{2,1,0:T(4,128)(2,1)} %get-tuple-element.1510) | copy-start | bytes 786436
  52.6 1.0 %copy-start.1 = (bf16[256,4,128]{2,1,0:T(4,128)(2,1)S(1)}, bf16[256,4,128]{2,1,0:T(4,128)(2,1)}, u32[]{:S(2)}) copy-start(bf16[256,4,128]{2,1,0:T(4,128)(2,1)} %get-tuple-element.1544) | copy-start | bytes 786436
  56.5 7.4 %all-to-all-start.2 = ((bf16[4,2,4096]{2,1,0:T(2,128)(2,1)}), bf16[4,2,4096]{2,1,0:T(2,128)(2,1)S(1)}, u32[]{:S(2)}, u32[]{:S(2)}) async-start(bf16[4,2,4096]{2,1,0:T(2,128)(2,1)} %reshape.467), calls=%async_computation.2 | async-start | bytes 131072 | tf_op jit(solution)/shard_map/all_to_all | solution.py:206
  63.9 7.4 %all-to-all-start.3 = ((bf16[4,2,4096]{2,1,0:T(2,128)(2,1)}), bf16[4,2,4096]{2,1,0:T(2,128)(2,1)S(1)}, u32[]{:S(2)}, u32[]{:S(2)}) async-start(bf16[4,2,4096]{2,1,0:T(2,128)(2,1)} %reshape.469), calls=%async_computation.3 | async-start | bytes 131072 | tf_op jit(solution)/shard_map/all_to_all | solution.py:207
where the time goes:
time: 72.8 us; the launch traced here: 72.1 us
  starting transfers between devices  21.6 us (30%)
  waiting for transfers between devices  13.9 us (19%)
  other arithmetic  13.1 us (18%)
  local copies, waits for them, and re-layouts  9.34 us (13%)
  matrix products  7.29 us (10%)
  loops' own time  5.9 us (8%)
  between operations  0.94 us (1%)
    ppermute x4, starting transfers between devices, shifted(): lax.ppermute(value, axis, [(i, (i + by) % size) for i in range(size)])  7.48 us
    unnamed x22, local copies, waits for them, and re-layouts  5.77 us
    ppermute x4, waiting for transfers between devices, shifted(): lax.ppermute(value, axis, [(i, (i + by) % size) for i in range(size)])  5.27 us
    all_to_all x1, starting transfers between devices, per_device(): lax.all_to_all(value_vectors, 'head', split_axis=1, concat_axis=0, tiled=...  4.26 us
    all_to_all x1, starting transfers between devices, per_device(): lax.all_to_all(key_vectors, 'head', split_axis=1, concat_axis=0, tiled=True)  3.29 us
    all_to_all x1, starting transfers between devices, per_device(): lax.all_to_all(key_home_grad, 'head', split_axis=0, concat_axis=1, tiled=...  3.28 us
    all_to_all x1, starting transfers between devices, per_device(): lax.all_to_all(value_home_grad, 'head', split_axis=0, concat_axis=1, tile...  3.28 us
    reduce_or x4, other arithmetic, forward_tile(): jnp.any(allowed)  3.08 us
  transfers between devices with their start and end apart: 8, of which 6 were waited for; matrix products, arithmetic and copies ran while one was open for 12% of the time, Pallas kernels for 0%

commit v1 on v0

--- a/solution.py
+++ b/solution.py
@@ -1,8 +1,11 @@
+import functools
 import math
 
 import jax
 import jax.numpy as jnp
 from jax import lax
+from jax.experimental import pallas as pl
+from jax.experimental.pallas import tpu as pltpu
 from jax.sharding import PartitionSpec as P
 
 GROUPS = 4
@@ -209,9 +212,282 @@
     return (attended, query_grad, key_grad, value_grad)
 
 
+def pair_groups(devices, head_devices, sizes):
+    _, kv_rows, kv_heads, head_dim = sizes
+    return devices == 2 * GROUPS and kv_heads == head_devices and head_dim == 128
+
+
+NT = (((1,), (1,)), ((), ()))
+NN = (((1,), (0,)), ((), ()))
+
+
+def dot(left, right, dims=NN):
+    return lax.dot_general(left, right, dims, preferred_element_type=jnp.float32)
+
+
+def fused_kernel(
+    devices,
+    peers,
+    heads,
+    q_hbm,
+    k_ref,
+    v_ref,
+    g_hbm,
+    att_hbm,
+    dq_hbm,
+    dk_ref,
+    dv_ref,
+    q_ref,
+    g_ref,
+    att_ref,
+    dq_ref,
+    spread,
+    kv_send,
+    kv,
+    kv_t,
+    w_ref,
+    ds_ref,
+    g_send,
+    g_land,
+    load_sem,
+    store_sem,
+    kv_send_sem,
+    kv_recv_sem,
+    g_send_sem,
+    g_recv_sem,
+):
+    s = lax.axis_index("seq")
+    h = lax.axis_index("head")
+    after = lax.rem(s + 1, devices)
+    before = lax.rem(s + devices - 1, devices)
+    rows = q_ref.shape[0]
+    head_dim = q_ref.shape[1]
+    tokens = rows // heads
+    piece = tokens // peers
+    chunk = 256
+    chunk_tok = chunk // heads
+    chunks = rows // chunk
+    scale = 1.0 / math.sqrt(head_dim)
+    log2e = 1.4426950408889634
+
+    def peer(d):
+        return lax.rem(h + d, peers)
+
+    barrier = pltpu.get_barrier_semaphore()
+    for d in range(peers):
+        if d:
+            pl.semaphore_signal(barrier, inc=1, device_id=(s, peer(d)), device_id_type=MESH)
+        pl.semaphore_signal(barrier, inc=1, device_id=(after, peer(d)), device_id_type=MESH)
+        pl.semaphore_signal(barrier, inc=1, device_id=(before, peer(d)), device_id_type=MESH)
+
+    load_q = pltpu.make_async_copy(q_hbm, q_ref, load_sem.at[0])
+    load_g = pltpu.make_async_copy(g_hbm, g_ref, load_sem.at[1])
+    load_q.start()
+    load_g.start()
+
+    spread[0] = k_ref[...].astype(jnp.float32)
+    spread[1] = v_ref[...].astype(jnp.float32)
+    for p in range(peers):
+        for which in range(2):
+            kv_send[p, which] = spread[which, pl.ds(p, piece, stride=peers), :].astype(jnp.bfloat16)
+
+    mine = pl.ds(pl.multiple_of(h * piece, piece), piece)
+    mine_own = pl.ds(pl.multiple_of(tokens + h * piece, piece), piece)
+    pl.semaphore_wait(barrier, 3 * peers - 1)
+
+    own_copies = []
+    prev_copies = []
+    for d in range(1, peers):
+        own_copies.append(
+            pltpu.make_async_remote_copy(
+                src_ref=kv_send.at[peer(d)],
+                dst_ref=kv.at[:, mine_own, :],
+                send_sem=kv_send_sem.at[d],
+                recv_sem=kv_recv_sem.at[d],
+                device_id=(s, peer(d)),
+                device_id_type=MESH,
+            )
+        )
+    for d in range(peers):
+        prev_copies.append(
+            pltpu.make_async_remote_copy(
+                src_ref=kv_send.at[peer(d)],
+                dst_ref=kv.at[:, mine, :],
+                send_sem=kv_send_sem.at[peers + d],
+                recv_sem=kv_recv_sem.at[peers + d],
+                device_id=(after, peer(d)),
+                device_id_type=MESH,
+            )
+        )
+    for copy in own_copies + prev_copies:
+        copy.start()
+    kv[:, mine_own, :] = kv_send[h]
+    for copy in own_copies + prev_copies:
+        copy.wait()
+    load_q.wait()
+    load_g.wait()
+
+    for which in range(2):
+        kv_t[which] = kv[which].T
+
+    lane = lax.broadcasted_iota(jnp.int32, (1, chunk), 1)
+    sees_prev = (lax.rem(lane, heads) // (heads // 2)) == lax.rem(s + 1, 2)
+    diag_key = lax.broadcasted_iota(jnp.int32, (chunk_tok, chunk), 0)
+    diag_tok = lax.broadcasted_iota(jnp.int32, (chunk_tok, chunk), 1) // heads
+    diag = diag_key <= diag_tok
+    unit = scale * log2e
+
+    for a in range(chunks):
+        here = pl.ds(a * chunk, chunk)
+        own_keys = chunk_tok * (a + 1)
+        total_keys = tokens + own_keys
+        q_a = q_ref[here, :]
+        g_a = g_ref[here, :]
+        scores = dot(kv[0, :total_keys, :], q_a, NT) * unit
+        prev = scores[:tokens]
+        full = scores[tokens : total_keys - chunk_tok]
+        edge = jnp.where(diag, scores[total_keys - chunk_tok :], -jnp.inf)
+        top = jnp.where(sees_prev, jnp.max(prev, axis=0, keepdims=True), -jnp.inf)
+        top = jnp.maximum(top, jnp.max(edge, axis=0, keepdims=True))
+        if a:
+            top = jnp.maximum(top, jnp.max(full, axis=0, keepdims=True))
+        top_prev = jnp.where(sees_prev, top, 1e30)
+        parts = [jnp.exp2(prev - top_prev)]
+        if a:
+            parts.append(jnp.exp2(full - top))
+        parts.append(jnp.exp2(edge - top))
+        probs = jnp.concatenate(parts, axis=0)
+        inverse = 1.0 / jnp.sum(probs, axis=0, keepdims=True)
+        probs = probs * inverse
+        w_ref[:total_keys, here] = probs.astype(jnp.bfloat16)
+        prob_grad = dot(kv[1, :total_keys, :], g_a, NT)
+        delta = jnp.sum(probs * prob_grad, axis=0, keepdims=True)
+        ds_ref[:total_keys, here] = (probs * (prob_grad - delta)).astype(jnp.bfloat16)
+        limit = tokens + -(-own_keys // 128) * 128
+        if limit > total_keys:
+            blank = jnp.zeros((limit - total_keys, chunk), jnp.bfloat16)
+            w_ref[total_keys:limit, here] = blank
+            ds_ref[total_keys:limit, here] = blank
+
+    def send_grads(which, slot, target, d):
+        return pltpu.make_async_remote_copy(
+            src_ref=g_send.at[which, :, pl.ds(pl.multiple_of(peer(d) * piece, piece), piece), :],
+            dst_ref=g_land.at[which, h],
+            send_sem=g_send_sem.at[slot],
+            recv_sem=g_recv_sem.at[slot],
+            device_id=(target, peer(d)),
+            device_id_type=MESH,
+        )
+
+    g_send[0, 1] = dot(w_ref[:tokens, :], g_ref[...]).astype(jnp.bfloat16)
+    g_send[0, 0] = (dot(ds_ref[:tokens, :], q_ref[...]) * scale).astype(jnp.bfloat16)
+    grad_copies = [send_grads(0, peers + d, before, d) for d in range(peers)]
+    for copy in grad_copies:
+        copy.start()
+
+    for low in range(0, tokens, 128):
+        keys = slice(tokens + low, tokens + low + 128)
+        first = low * heads
+        g_send[1, 1, low : low + 128] = dot(w_ref[keys, first:], g_ref[first:, :]).astype(jnp.bfloat16)
+        g_send[1, 0, low : low + 128] = (dot(ds_ref[keys, first:], q_ref[first:, :]) * scale).astype(
+            jnp.bfloat16
+        )
+    own_grads = [send_grads(1, d, s, d) for d in range(1, peers)]
+    for copy in own_grads:
+        copy.start()
+    g_land[1, h] = g_send[1, :, mine, :]
+
+    stores = []
+    for a in range(chunks):
+        here = pl.ds(a * chunk, chunk)
+        limit = tokens + -(-(chunk_tok * (a + 1)) // 128) * 128
+        att_ref[here, :] = dot(kv_t[1, :, :limit], w_ref[:limit, here]).astype(jnp.bfloat16).T
+        dq_ref[here, :] = (dot(kv_t[0, :, :limit], ds_ref[:limit, here]) * scale).astype(jnp.bfloat16).T
+    stores = [
+        pltpu.make_async_copy(att_ref, att_hbm, store_sem.at[0]),
+        pltpu.make_async_copy(dq_ref, dq_hbm, store_sem.at[1]),
+    ]
+    for copy in stores:
+        copy.start()
+
+    for copy in grad_copies + own_grads:
+        copy.wait()
+    for which, out in ((0, dk_ref), (1, dv_ref)):
+        for p in range(peers):
+            spread[which, pl.ds(p, piece, stride=peers), :] = g_land[0, p, which].astype(
+                jnp.float32
+            ) + g_land[1, p, which].astype(jnp.float32)
+        out[...] = spread[which].astype(jnp.bfloat16)
+    for copy in stores:
+        copy.wait()
+
+
+MESH = pl.DeviceIdType.MESH
+
+
+def fused_device(queries, key_vectors, value_vectors, out_grad):
+    devices = lax.axis_size("seq")
+    peers = lax.axis_size("head")
+    tokens, heads, head_dim = queries.shape
+    piece, kv_heads, _ = key_vectors.shape
+    rows = tokens * heads
+    kv_rows = piece * kv_heads
+    bf16, f32 = jnp.bfloat16, jnp.float32
+    big = jax.ShapeDtypeStruct((rows, head_dim), bf16)
+    small = jax.ShapeDtypeStruct((kv_rows, head_dim), bf16)
+    hbm = pl.BlockSpec(memory_space=pl.ANY)
+    vmem = pl.BlockSpec(memory_space=pltpu.VMEM)
+    dma = pltpu.SemaphoreType.DMA
+    att, dq, dk, dv = pl.pallas_call(
+        functools.partial(fused_kernel, devices, peers, heads),
+        out_shape=(big, big, small, small),
+        in_specs=[hbm, vmem, vmem, hbm],
+        out_specs=(hbm, hbm, vmem, vmem),
+        scratch_shapes=[
+            pltpu.VMEM((rows, head_dim), bf16),
+            pltpu.VMEM((rows, head_dim), bf16),
+            pltpu.VMEM((rows, head_dim), bf16),
+            pltpu.VMEM((rows, head_dim), bf16),
+            pltpu.VMEM((2, kv_rows, head_dim), f32),
+            pltpu.VMEM((peers, 2, piece, head_dim), bf16),
+            pltpu.VMEM((2, 2 * tokens, head_dim), bf16),
+            pltpu.VMEM((2, head_dim, 2 * tokens), bf16),
+            pltpu.VMEM((2 * tokens, rows), bf16),
+            pltpu.VMEM((2 * tokens, rows), bf16),
+            pltpu.VMEM((2, 2, tokens, head_dim), bf16),
+            pltpu.VMEM((2, peers, 2, piece, head_dim), bf16),
+            dma((2,)),
+            dma((2,)),
+            dma((2 * peers,)),
+            dma((2 * peers,)),
+            dma((2 * peers,)),
+            dma((2 * peers,)),
+        ],
+        compiler_params=pltpu.CompilerParams(
+            collective_id=0, has_side_effects=True, vmem_limit_bytes=48 * 1024 * 1024
+        ),
+    )(
+        queries.reshape(rows, head_dim),
+        key_vectors.reshape(kv_rows, head_dim),
+        value_vectors.reshape(kv_rows, head_dim),
+        out_grad.reshape(rows, head_dim),
+    )
+    return (
+        att.reshape(queries.shape),
+        dq.reshape(queries.shape),
+        dk.reshape(key_vectors.shape),
+        dv.reshape(value_vectors.shape),
+    )
+
+
 def solution(mesh):
-    return jax.shard_map(
-        per_device,
+    def step(queries, key_vectors, value_vectors, out_grad):
+        sizes = (queries.shape[0], queries.shape[1], key_vectors.shape[1], queries.shape[2])
+        body = fused_device if pair_groups(mesh.shape["seq"], mesh.shape["head"], sizes) else per_device
+        return run(body)(queries, key_vectors, value_vectors, out_grad)
+
+    run = lambda body: jax.shard_map(
+        body,
         mesh=mesh,
         in_specs=(
             P("seq", "head", None),
@@ -227,3 +503,4 @@
         ),
         check_vma=False,
     )
+    return step

time: 72.8 us -> 27.2 us (0.37)
  starting transfers between devices: 21.6 us -> 0 us
  Pallas kernels: 0 us -> 19.7 us
  waiting for transfers between devices: 13.9 us -> 0 us
  other arithmetic: 13.1 us -> 0 us
  matrix products: 7.29 us -> 0 us
  loops' own time: 5.9 us -> 0 us
  local copies, waits for them, and re-layouts: 9.34 us -> 6.6 us
    pallas_call x0 -> x1, Pallas kernels: none -> 19.7 us  [fused_device(): pl.pallas_call(functools.partial(fused_kernel, devices, peers, heads), ou...]
    all_to_all x4 -> x0, starting transfers between devices: 14.1 us -> none  [the longest x1 4.26 us: per_device(): lax.all_to_all(value_vectors, 'head', split_axis=1, concat_axis=0, tiled=...]
    all_to_all x4 -> x0, waiting for transfers between devices: 8.62 us -> none  [the longest x1 2.73 us: per_device(): lax.all_to_all(key_home_grad, 'head', split_axis=0, concat_axis=1, tiled=...]
    ppermute x4 -> x0, starting transfers between devices: 7.48 us -> none  [shifted(): lax.ppermute(value, axis, [(i, (i + by) % size) for i in range(size)])]
    dot_general x21 -> x0, matrix products: 7.29 us -> none  [the longest x6 2.07 us: scores_of(): jnp.einsum('ihd,td->hit', q_parts[which_half], key_blk, preferred_element...]
    reduce_or x8 -> x0, other arithmetic: 6.17 us -> none  [the longest x4 3.08 us: forward_tile(): jnp.any(allowed)]
    another operation x10 -> x0, loops' own time: 5.9 us -> none  [the longest x1 2.8 us: per_device(): lax.fori_loop(0, group_span, window_backward, ((zero_query, zero_query),...]
    ppermute x4 -> x0, waiting for transfers between devices: 5.27 us -> none  [shifted(): lax.ppermute(value, axis, [(i, (i + by) % size) for i in range(size)])]
  transfers between devices with their start and end apart: 8 -> 0, of which waited for: 6 -> 0; matrix products, arithmetic and copies ran while one was open for 12% -> 0% of each run, Pallas kernels for 0% -> 0%
where the time goes in v1:
time: 27.2 us; the launch traced here: 26.9 us
  Pallas kernels  19.7 us (72%)
  local copies, waits for them, and re-layouts  6.6 us (24%)
  between operations  0.65 us (2%)
    pallas_call x1, Pallas kernels, fused_device(): pl.pallas_call(functools.partial(fused_kernel, devices, peers, heads), ou...  19.7 us
    unnamed x12, local copies, waits for them, and re-layouts  6.6 us

profile of v1, /device:TPU:0, one launch (start us, length us, event | category | flops | bytes accessed | tf_op | source)
XLA Modules:
  0.0 26.9 jit_solution(4682468730412887506)
XLA Ops:
  0.6 0.0 copy-start
  0.6 1.0 %copy-done = bf16[256,8,128]{2,1,0:T(8,128)(2,1)S(1)} copy-done((bf16[256,8,128]{2,1,0:T(8,128)(2,1)S(1)}, bf16[256,8,128]{2,1,0:T(8,128)(2,1)}, u32[]{:S(2)}) %copy-start) | copy-done | bytes 524312
  1.7 0.0 copy-start.1
  1.7 1.0 %copy-done.1 = bf16[256,8,128]{2,1,0:T(8,128)(2,1)S(1)} copy-done((bf16[256,8,128]{2,1,0:T(8,128)(2,1)S(1)}, bf16[256,8,128]{2,1,0:T(8,128)(2,1)}, u32[]{:S(2)}) %copy-start.1) | copy-done | bytes 524312
  2.7 0.0 copy-start.2
  2.7 0.8 %copy-done.2 = bf16[64,4,128]{2,1,0:T(4,128)(2,1)S(1)} copy-done((bf16[64,4,128]{2,1,0:T(4,128)(2,1)S(1)}, bf16[64,4,128]{2,1,0:T(4,128)(2,1)}, u32[]{:S(2)}) %copy-start.2) | copy-done | bytes 65560
  3.6 0.0 copy-start.3
  3.6 0.8 %copy-done.3 = bf16[64,4,128]{2,1,0:T(4,128)(2,1)S(1)} copy-done((bf16[64,4,128]{2,1,0:T(4,128)(2,1)S(1)}, bf16[64,4,128]{2,1,0:T(4,128)(2,1)}, u32[]{:S(2)}) %copy-start.3) | copy-done | bytes 65560
  4.4 19.7 %shard_map.75 = (bf16[2048,128]{1,0:T(8,128)(2,1)S(1)}, bf16[2048,128]{1,0:T(8,128)(2,1)S(1)}, bf16[256,128]{1,0:T(8,128)(2,1)S(1)}, bf16[256,128]{1,0:T(8,128)(2,1)S(1)}) custom-call(bf16[2048,128]{1,0:T(8,128)(2,1)S(1)} %bitcast.8, bf16[256,128]{1,0:T(8,128)(2,1)S(1)} %bitcast.12, bf16[256,128]{1,0:T(8,128)(2,1)S(1)} %bitcast.13, bf16[2048,128]{1,0:T(8,128)(2,1)S(1)} %bitcast.9), custom_call_target="tpu_custom_call" | custom-call | tf_op jit(solution)/shard_map/pallas_call | solution.py:441
  24.1 0.8 %copy.12 = bf16[256,8,128]{2,1,0:T(8,128)(2,1)} copy(bf16[256,8,128]{2,1,0:T(8,128)(2,1)S(1)} %bitcast.11) | data formatting | bytes 1048576
  24.9 0.8 %copy.13 = bf16[256,8,128]{2,1,0:T(8,128)(2,1)} copy(bf16[256,8,128]{2,1,0:T(8,128)(2,1)S(1)} %bitcast.10) | data formatting | bytes 1048576
  25.7 0.6 %copy.14 = bf16[64,4,128]{2,1,0:T(4,128)(2,1)} copy(bf16[64,4,128]{2,1,0:T(4,128)(2,1)S(1)} %bitcast.15) | data formatting | bytes 131072
  26.3 0.6 %copy.15 = bf16[64,4,128]{2,1,0:T(4,128)(2,1)} copy(bf16[64,4,128]{2,1,0:T(4,128)(2,1)S(1)} %bitcast.14) | data formatting | bytes 131072
Async XLA Ops:
  0.6 1.0 %copy-start = (bf16[256,8,128]{2,1,0:T(8,128)(2,1)S(1)}, bf16[256,8,128]{2,1,0:T(8,128)(2,1)}, u32[]{:S(2)}) copy-start(bf16[256,8,128]{2,1,0:T(8,128)(2,1)} %param.4) | copy-start | bytes 1572868
  1.7 1.0 %copy-start.1 = (bf16[256,8,128]{2,1,0:T(8,128)(2,1)S(1)}, bf16[256,8,128]{2,1,0:T(8,128)(2,1)}, u32[]{:S(2)}) copy-start(bf16[256,8,128]{2,1,0:T(8,128)(2,1)} %param.7) | copy-start | bytes 1572868
  2.7 0.8 %copy-start.2 = (bf16[64,4,128]{2,1,0:T(4,128)(2,1)S(1)}, bf16[64,4,128]{2,1,0:T(4,128)(2,1)}, u32[]{:S(2)}) copy-start(bf16[64,4,128]{2,1,0:T(4,128)(2,1)} %param.5) | copy-start | bytes 196612
  3.6 0.8 %copy-start.3 = (bf16[64,4,128]{2,1,0:T(4,128)(2,1)S(1)}, bf16[64,4,128]{2,1,0:T(4,128)(2,1)}, u32[]{:S(2)}) copy-start(bf16[64,4,128]{2,1,0:T(4,128)(2,1)} %param.6) | copy-start | bytes 196612

commit v2 on v1

--- a/solution.py
+++ b/solution.py
@@ -230,27 +230,28 @@
     peers,
     heads,
     q_hbm,
-    k_ref,
-    v_ref,
+    k_hbm,
+    v_hbm,
     g_hbm,
-    att_hbm,
-    dq_hbm,
+    att_ref,
+    dq_ref,
     dk_ref,
     dv_ref,
     q_ref,
     g_ref,
-    att_ref,
-    dq_ref,
+    kv_in,
     spread,
     kv_send,
     kv,
     kv_t,
+    p_own,
+    dp_own,
+    stats,
     w_ref,
     ds_ref,
     g_send,
     g_land,
     load_sem,
-    store_sem,
     kv_send_sem,
     kv_recv_sem,
     g_send_sem,
@@ -268,123 +269,146 @@
     chunk_tok = chunk // heads
     chunks = rows // chunk
     scale = 1.0 / math.sqrt(head_dim)
-    log2e = 1.4426950408889634
+    unit = scale * 1.4426950408889634
 
     def peer(d):
         return lax.rem(h + d, peers)
 
+    loads = [
+        pltpu.make_async_copy(src, dst, load_sem.at[i])
+        for i, (src, dst) in enumerate(
+            ((k_hbm, kv_in.at[0]), (v_hbm, kv_in.at[1]), (q_hbm, q_ref), (g_hbm, g_ref))
+        )
+    ]
+    for copy in loads:
+        copy.start()
+
     barrier = pltpu.get_barrier_semaphore()
     for d in range(peers):
+        pl.semaphore_signal(barrier, inc=1, device_id=(before, peer(d)), device_id_type=MESH)
+        pl.semaphore_signal(barrier, inc=1, device_id=(after, peer(d)), device_id_type=MESH)
         if d:
             pl.semaphore_signal(barrier, inc=1, device_id=(s, peer(d)), device_id_type=MESH)
-        pl.semaphore_signal(barrier, inc=1, device_id=(after, peer(d)), device_id_type=MESH)
-        pl.semaphore_signal(barrier, inc=1, device_id=(before, peer(d)), device_id_type=MESH)
-
-    load_q = pltpu.make_async_copy(q_hbm, q_ref, load_sem.at[0])
-    load_g = pltpu.make_async_copy(g_hbm, g_ref, load_sem.at[1])
-    load_q.start()
-    load_g.start()
-
-    spread[0] = k_ref[...].astype(jnp.float32)
-    spread[1] = v_ref[...].astype(jnp.float32)
-    for p in range(peers):
-        for which in range(2):
+
+    for which in range(2):
+        loads[which].wait()
+        spread[which] = kv_in[which].astype(jnp.float32)
+        for p in range(peers):
             kv_send[p, which] = spread[which, pl.ds(p, piece, stride=peers), :].astype(jnp.bfloat16)
 
     mine = pl.ds(pl.multiple_of(h * piece, piece), piece)
     mine_own = pl.ds(pl.multiple_of(tokens + h * piece, piece), piece)
     pl.semaphore_wait(barrier, 3 * peers - 1)
 
-    own_copies = []
-    prev_copies = []
-    for d in range(1, peers):
-        own_copies.append(
-            pltpu.make_async_remote_copy(
-                src_ref=kv_send.at[peer(d)],
-                dst_ref=kv.at[:, mine_own, :],
-                send_sem=kv_send_sem.at[d],
-                recv_sem=kv_recv_sem.at[d],
-                device_id=(s, peer(d)),
-                device_id_type=MESH,
+    def send_kv(slot, src, dst, target, d):
+        return pltpu.make_async_remote_copy(
+            src_ref=src,
+            dst_ref=dst,
+            send_sem=kv_send_sem.at[slot],
+            recv_sem=kv_recv_sem.at[slot],
+            device_id=(target, peer(d)),
+            device_id_type=MESH,
+        )
+
+    own_copies = [
+        send_kv(d, kv_send.at[peer(d)], kv.at[:, mine_own, :], s, d) for d in range(1, peers)
+    ]
+    prev_copies = [
+        [
+            send_kv(
+                (1 + which) * peers + d, kv_send.at[peer(d), which], kv.at[which, mine, :], after, d
             )
-        )
-    for d in range(peers):
-        prev_copies.append(
-            pltpu.make_async_remote_copy(
-                src_ref=kv_send.at[peer(d)],
-                dst_ref=kv.at[:, mine, :],
-                send_sem=kv_send_sem.at[peers + d],
-                recv_sem=kv_recv_sem.at[peers + d],
-                device_id=(after, peer(d)),
-                device_id_type=MESH,
-            )
-        )
-    for copy in own_copies + prev_copies:
+            for d in range(peers)
+        ]
+        for which in range(2)
+    ]
+    for copy in own_copies + prev_copies[0] + prev_copies[1]:
         copy.start()
     kv[:, mine_own, :] = kv_send[h]
-    for copy in own_copies + prev_copies:
+    loads[2].wait()
+    loads[3].wait()
+    for copy in own_copies:
         copy.wait()
-    load_q.wait()
-    load_g.wait()
-
-    for which in range(2):
-        kv_t[which] = kv[which].T
 
     lane = lax.broadcasted_iota(jnp.int32, (1, chunk), 1)
     sees_prev = (lax.rem(lane, heads) // (heads // 2)) == lax.rem(s + 1, 2)
     diag_key = lax.broadcasted_iota(jnp.int32, (chunk_tok, chunk), 0)
     diag_tok = lax.broadcasted_iota(jnp.int32, (chunk_tok, chunk), 1) // heads
     diag = diag_key <= diag_tok
-    unit = scale * log2e
 
     for a in range(chunks):
         here = pl.ds(a * chunk, chunk)
         own_keys = chunk_tok * (a + 1)
-        total_keys = tokens + own_keys
-        q_a = q_ref[here, :]
-        g_a = g_ref[here, :]
-        scores = dot(kv[0, :total_keys, :], q_a, NT) * unit
-        prev = scores[:tokens]
-        full = scores[tokens : total_keys - chunk_tok]
-        edge = jnp.where(diag, scores[total_keys - chunk_tok :], -jnp.inf)
-        top = jnp.where(sees_prev, jnp.max(prev, axis=0, keepdims=True), -jnp.inf)
-        top = jnp.maximum(top, jnp.max(edge, axis=0, keepdims=True))
+        inner = own_keys - chunk_tok
+        scores = dot(kv[0, tokens : tokens + own_keys, :], q_ref[here, :], NT) * unit
+        edge = jnp.where(diag, scores[inner:], -jnp.inf)
+        top = jnp.max(edge, axis=0, keepdims=True)
         if a:
-            top = jnp.maximum(top, jnp.max(full, axis=0, keepdims=True))
-        top_prev = jnp.where(sees_prev, top, 1e30)
-        parts = [jnp.exp2(prev - top_prev)]
-        if a:
-            parts.append(jnp.exp2(full - top))
-        parts.append(jnp.exp2(edge - top))
-        probs = jnp.concatenate(parts, axis=0)
-        inverse = 1.0 / jnp.sum(probs, axis=0, keepdims=True)
-        probs = probs * inverse
-        w_ref[:total_keys, here] = probs.astype(jnp.bfloat16)
-        prob_grad = dot(kv[1, :total_keys, :], g_a, NT)
-        delta = jnp.sum(probs * prob_grad, axis=0, keepdims=True)
-        ds_ref[:total_keys, here] = (probs * (prob_grad - delta)).astype(jnp.bfloat16)
-        limit = tokens + -(-own_keys // 128) * 128
-        if limit > total_keys:
-            blank = jnp.zeros((limit - total_keys, chunk), jnp.bfloat16)
-            w_ref[total_keys:limit, here] = blank
-            ds_ref[total_keys:limit, here] = blank
-
-    def send_grads(which, slot, target, d):
+            top = jnp.maximum(top, jnp.max(scores[:inner], axis=0, keepdims=True))
+            edge = jnp.concatenate([scores[:inner], edge], axis=0)
+        probs = jnp.exp2(edge - top)
+        prob_grad = dot(kv[1, tokens : tokens + own_keys, :], g_ref[here, :], NT)
+        p_own[:own_keys, here] = probs
+        dp_own[:own_keys, here] = prob_grad
+        stats[0:1, here] = top
+        stats[1:2, here] = jnp.sum(probs, axis=0, keepdims=True)
+        stats[2:3, here] = jnp.sum(probs * prob_grad, axis=0, keepdims=True)
+
+    def send_grads(block, which, slot, target, d):
         return pltpu.make_async_remote_copy(
-            src_ref=g_send.at[which, :, pl.ds(pl.multiple_of(peer(d) * piece, piece), piece), :],
-            dst_ref=g_land.at[which, h],
+            src_ref=g_send.at[block, which, pl.ds(pl.multiple_of(peer(d) * piece, piece), piece), :],
+            dst_ref=g_land.at[block, h, which],
             send_sem=g_send_sem.at[slot],
             recv_sem=g_recv_sem.at[slot],
             device_id=(target, peer(d)),
             device_id_type=MESH,
         )
 
+    for copy in prev_copies[0]:
+        copy.wait()
+    for a in range(chunks):
+        here = pl.ds(a * chunk, chunk)
+        scores = dot(kv[0, :tokens, :], q_ref[here, :], NT) * unit
+        top_own = stats[0:1, here]
+        top = jnp.where(sees_prev, jnp.max(scores, axis=0, keepdims=True), -jnp.inf)
+        top = jnp.maximum(top, top_own)
+        probs = jnp.exp2(scores - jnp.where(sees_prev, top, 1e30))
+        factor = jnp.exp2(top_own - top)
+        inverse = 1.0 / (jnp.sum(probs, axis=0, keepdims=True) + factor * stats[1:2, here])
+        w_ref[:tokens, here] = (probs * inverse).astype(jnp.bfloat16)
+        stats[3:4, here] = factor * inverse
     g_send[0, 1] = dot(w_ref[:tokens, :], g_ref[...]).astype(jnp.bfloat16)
+    prev_v_grads = [send_grads(0, 1, peers + d, before, d) for d in range(peers)]
+    for copy in prev_v_grads:
+        copy.start()
+
+    for copy in prev_copies[1]:
+        copy.wait()
+    for a in range(chunks):
+        here = pl.ds(a * chunk, chunk)
+        weights = w_ref[:tokens, here].astype(jnp.float32)
+        prob_grad = dot(kv[1, :tokens, :], g_ref[here, :], NT)
+        delta = jnp.sum(weights * prob_grad, axis=0, keepdims=True) + stats[3:4, here] * stats[2:3, here]
+        stats[4:5, here] = delta
+        ds_ref[:tokens, here] = (weights * (prob_grad - delta)).astype(jnp.bfloat16)
     g_send[0, 0] = (dot(ds_ref[:tokens, :], q_ref[...]) * scale).astype(jnp.bfloat16)
-    grad_copies = [send_grads(0, peers + d, before, d) for d in range(peers)]
-    for copy in grad_copies:
+    prev_k_grads = [send_grads(0, 0, d, before, d) for d in range(peers)]
+    for copy in prev_k_grads:
         copy.start()
 
+    for a in range(chunks):
+        here = pl.ds(a * chunk, chunk)
+        own_keys = chunk_tok * (a + 1)
+        weights = p_own[:own_keys, here] * stats[3:4, here]
+        w_ref[tokens : tokens + own_keys, here] = weights.astype(jnp.bfloat16)
+        ds_ref[tokens : tokens + own_keys, here] = (
+            weights * (dp_own[:own_keys, here] - stats[4:5, here])
+        ).astype(jnp.bfloat16)
+        limit = -(-own_keys // 128) * 128
+        if limit > own_keys:
+            blank = jnp.zeros((limit - own_keys, chunk), jnp.bfloat16)
+            w_ref[tokens + own_keys : tokens + limit, here] = blank
+            ds_ref[tokens + own_keys : tokens + limit, here] = blank
     for low in range(0, tokens, 128):
         keys = slice(tokens + low, tokens + low + 128)
         first = low * heads
@@ -392,25 +416,24 @@
         g_send[1, 0, low : low + 128] = (dot(ds_ref[keys, first:], q_ref[first:, :]) * scale).astype(
             jnp.bfloat16
         )
-    own_grads = [send_grads(1, d, s, d) for d in range(1, peers)]
+    own_grads = [
+        send_grads(1, which, (2 + which) * peers + d, s, d)
+        for which in range(2)
+        for d in range(1, peers)
+    ]
     for copy in own_grads:
         copy.start()
     g_land[1, h] = g_send[1, :, mine, :]
 
-    stores = []
+    for which in range(2):
+        kv_t[which] = kv[which].T
     for a in range(chunks):
         here = pl.ds(a * chunk, chunk)
         limit = tokens + -(-(chunk_tok * (a + 1)) // 128) * 128
         att_ref[here, :] = dot(kv_t[1, :, :limit], w_ref[:limit, here]).astype(jnp.bfloat16).T
         dq_ref[here, :] = (dot(kv_t[0, :, :limit], ds_ref[:limit, here]) * scale).astype(jnp.bfloat16).T
-    stores = [
-        pltpu.make_async_copy(att_ref, att_hbm, store_sem.at[0]),
-        pltpu.make_async_copy(dq_ref, dq_hbm, store_sem.at[1]),
-    ]
-    for copy in stores:
-        copy.start()
-
-    for copy in grad_copies + own_grads:
+
+    for copy in prev_v_grads + prev_k_grads + own_grads:
         copy.wait()
     for which, out in ((0, dk_ref), (1, dv_ref)):
         for p in range(peers):
@@ -418,7 +441,16 @@
                 jnp.float32
             ) + g_land[1, p, which].astype(jnp.float32)
         out[...] = spread[which].astype(jnp.bfloat16)
-    for copy in stores:
+
+
+def place_kernel(*refs):
+    count = (len(refs) - 1) // 2
+    copies = [
+        pltpu.make_async_copy(refs[i], refs[count + i], refs[-1].at[i]) for i in range(count)
+    ]
+    for copy in copies:
+        copy.start()
+    for copy in copies:
         copy.wait()
 
 
@@ -435,43 +467,52 @@
     bf16, f32 = jnp.bfloat16, jnp.float32
     big = jax.ShapeDtypeStruct((rows, head_dim), bf16)
     small = jax.ShapeDtypeStruct((kv_rows, head_dim), bf16)
-    hbm = pl.BlockSpec(memory_space=pl.ANY)
+    hbm = pl.BlockSpec(memory_space=pltpu.HBM)
     vmem = pl.BlockSpec(memory_space=pltpu.VMEM)
     dma = pltpu.SemaphoreType.DMA
-    att, dq, dk, dv = pl.pallas_call(
+    results = pl.pallas_call(
         functools.partial(fused_kernel, devices, peers, heads),
         out_shape=(big, big, small, small),
-        in_specs=[hbm, vmem, vmem, hbm],
-        out_specs=(hbm, hbm, vmem, vmem),
+        in_specs=[hbm] * 4,
+        out_specs=(vmem,) * 4,
         scratch_shapes=[
             pltpu.VMEM((rows, head_dim), bf16),
             pltpu.VMEM((rows, head_dim), bf16),
-            pltpu.VMEM((rows, head_dim), bf16),
-            pltpu.VMEM((rows, head_dim), bf16),
+            pltpu.VMEM((2, kv_rows, head_dim), bf16),
             pltpu.VMEM((2, kv_rows, head_dim), f32),
             pltpu.VMEM((peers, 2, piece, head_dim), bf16),
             pltpu.VMEM((2, 2 * tokens, head_dim), bf16),
             pltpu.VMEM((2, head_dim, 2 * tokens), bf16),
+            pltpu.VMEM((tokens, rows), f32),
+            pltpu.VMEM((tokens, rows), f32),
+            pltpu.VMEM((8, rows), f32),
             pltpu.VMEM((2 * tokens, rows), bf16),
             pltpu.VMEM((2 * tokens, rows), bf16),
             pltpu.VMEM((2, 2, tokens, head_dim), bf16),
             pltpu.VMEM((2, peers, 2, piece, head_dim), bf16),
-            dma((2,)),
-            dma((2,)),
-            dma((2 * peers,)),
-            dma((2 * peers,)),
-            dma((2 * peers,)),
-            dma((2 * peers,)),
+            dma((4,)),
+            dma((3 * peers,)),
+            dma((3 * peers,)),
+            dma((4 * peers,)),
+            dma((4 * peers,)),
         ],
         compiler_params=pltpu.CompilerParams(
-            collective_id=0, has_side_effects=True, vmem_limit_bytes=48 * 1024 * 1024
+            collective_id=0, has_side_effects=True, vmem_limit_bytes=40 * 1024 * 1024
         ),
     )(
-        queries.reshape(rows, head_dim),
-        key_vectors.reshape(kv_rows, head_dim),
-        value_vectors.reshape(kv_rows, head_dim),
-        out_grad.reshape(rows, head_dim),
+        *(
+            pltpu.with_memory_space_constraint(array.reshape(-1, head_dim), pltpu.HBM)
+            for array in (queries, key_vectors, value_vectors, out_grad)
+        )
     )
+    att, dq, dk, dv = pl.pallas_call(
+        place_kernel,
+        out_shape=(big, big, small, small),
+        in_specs=[vmem] * 4,
+        out_specs=(hbm,) * 4,
+        scratch_shapes=[dma((4,))],
+        compiler_params=pltpu.CompilerParams(vmem_limit_bytes=4 * 1024 * 1024),
+    )(*results)
     return (
         att.reshape(queries.shape),
         dq.reshape(queries.shape),

time: 27.2 us -> 20.6 us (0.76)
  local copies, waits for them, and re-layouts: 6.6 us -> 0 us
    unnamed x12 -> x0, local copies, waits for them, and re-layouts: 6.6 us -> none
    pallas_call x0 -> x1, Pallas kernels: none -> 1.03 us  [fused_device(): pl.pallas_call(place_kernel, out_shape=(big, big, small, small), in_specs...]
    pallas_call x1, Pallas kernels: 19.7 us -> 18.8 us  [fused_device(): pl.pallas_call(functools.partial(fused_kernel, devices, peers, heads), ou...]
where the time goes in v2:
time: 20.6 us; the launch traced here: 20.5 us
  Pallas kernels  19.8 us (96%)
  between operations  0.64 us (3%)
    pallas_call x1, Pallas kernels, fused_device(): pl.pallas_call(functools.partial(fused_kernel, devices, peers, heads), ou...  18.8 us
    pallas_call x1, Pallas kernels, fused_device(): pl.pallas_call(place_kernel, out_shape=(big, big, small, small), in_specs...  1.03 us

profile of v2, /device:TPU:0, one launch (start us, length us, event | category | flops | bytes accessed | tf_op | source)
XLA Modules:
  0.0 20.5 jit_solution(12189417032435845272)
XLA Ops:
  0.6 18.8 %shard_map.75 = (bf16[2048,128]{1,0:T(8,128)(2,1)S(1)}, bf16[2048,128]{1,0:T(8,128)(2,1)S(1)}, bf16[256,128]{1,0:T(8,128)(2,1)S(1)}, bf16[256,128]{1,0:T(8,128)(2,1)S(1)}) custom-call(bf16[2048,128]{1,0:T(8,128)(2,1)} %bitcast.8, bf16[256,128]{1,0:T(8,128)(2,1)} %bitcast.10, bf16[256,128]{1,0:T(8,128)(2,1)} %bitcast.11, bf16[2048,128]{1,0:T(8,128)(2,1)} %bitcast.9), custom_call_target="tpu_custom_call" | custom-call | tf_op jit(solution)/shard_map/pallas_call | solution.py:473
  19.4 1.0 %shard_map.76 = (bf16[2048,128]{1,0:T(8,128)(2,1)}, bf16[2048,128]{1,0:T(8,128)(2,1)}, bf16[256,128]{1,0:T(8,128)(2,1)}, bf16[256,128]{1,0:T(8,128)(2,1)}) custom-call(bf16[2048,128]{1,0:T(8,128)(2,1)S(1)} %get-tuple-element.12.refs_0_, bf16[2048,128]{1,0:T(8,128)(2,1)S(1)} %get-tuple-element.13.refs_1_, bf16[256,128]{1,0:T(8,128)(2,1)S(1)} %get-tuple-element.14.refs_2_, ...), custom_call_target="tpu_custom_call" | custom-call | tf_op jit(solution)/shard_map/pallas_call | solution.py:508

commit v3 on v2

--- a/solution.py
+++ b/solution.py
@@ -237,6 +237,8 @@
     dq_ref,
     dk_ref,
     dv_ref,
+    flat_in,
+    flat_out,
     q_ref,
     g_ref,
     kv_in,
@@ -249,6 +251,7 @@
     stats,
     w_ref,
     ds_ref,
+    own_sum,
     g_send,
     g_land,
     load_sem,
@@ -261,32 +264,28 @@
     h = lax.axis_index("head")
     after = lax.rem(s + 1, devices)
     before = lax.rem(s + devices - 1, devices)
-    rows = q_ref.shape[0]
-    head_dim = q_ref.shape[1]
+    rows, head_dim = att_ref.shape
     tokens = rows // heads
     piece = tokens // peers
+    half = heads // 2
     chunk = 256
-    chunk_tok = chunk // heads
-    chunks = rows // chunk
+    chunk_tok = chunk // half
+    chunks = tokens // chunk_tok
     scale = 1.0 / math.sqrt(head_dim)
     unit = scale * 1.4426950408889634
+    bases = (lax.rem(s, 2) * half, lax.rem(s + 1, 2) * half)
 
     def peer(d):
         return lax.rem(h + d, peers)
 
-    loads = [
-        pltpu.make_async_copy(src, dst, load_sem.at[i])
-        for i, (src, dst) in enumerate(
-            ((k_hbm, kv_in.at[0]), (v_hbm, kv_in.at[1]), (q_hbm, q_ref), (g_hbm, g_ref))
-        )
-    ]
+    raw = ((k_hbm, kv_in.at[0]), (v_hbm, kv_in.at[1]), (q_hbm, att_ref), (g_hbm, dq_ref))
+    loads = [pltpu.make_async_copy(src, dst, load_sem.at[i]) for i, (src, dst) in enumerate(raw)]
     for copy in loads:
         copy.start()
 
     barrier = pltpu.get_barrier_semaphore()
     for d in range(peers):
         pl.semaphore_signal(barrier, inc=1, device_id=(before, peer(d)), device_id_type=MESH)
-        pl.semaphore_signal(barrier, inc=1, device_id=(after, peer(d)), device_id_type=MESH)
         if d:
             pl.semaphore_signal(barrier, inc=1, device_id=(s, peer(d)), device_id_type=MESH)
 
@@ -298,7 +297,7 @@
 
     mine = pl.ds(pl.multiple_of(h * piece, piece), piece)
     mine_own = pl.ds(pl.multiple_of(tokens + h * piece, piece), piece)
-    pl.semaphore_wait(barrier, 3 * peers - 1)
+    pl.semaphore_wait(barrier, 2 * peers - 1)
 
     def send_kv(slot, src, dst, target, d):
         return pltpu.make_async_remote_copy(
@@ -322,37 +321,94 @@
         ]
         for which in range(2)
     ]
-    for copy in own_copies + prev_copies[0] + prev_copies[1]:
+    for copy in prev_copies[0] + own_copies + prev_copies[1]:
         copy.start()
     kv[:, mine_own, :] = kv_send[h]
-    loads[2].wait()
-    loads[3].wait()
+
+    def head_rows(part, c, j):
+        return pl.ds(c * chunk_tok * heads + bases[part] + j, chunk_tok, stride=heads)
+
+    for i, (raw_ref, ref) in enumerate(((att_ref, q_ref), (dq_ref, g_ref))):
+        loads[2 + i].wait()
+        flat_in[...] = raw_ref[...].astype(jnp.float32)
+        for part in range(2):
+            for c in range(chunks):
+                for j in range(half):
+                    low = c * chunk + j * chunk_tok
+                    ref[part, low : low + chunk_tok] = flat_in[head_rows(part, c, j), :].astype(
+                        jnp.bfloat16
+                    )
+
     for copy in own_copies:
         copy.wait()
-
-    lane = lax.broadcasted_iota(jnp.int32, (1, chunk), 1)
-    sees_prev = (lax.rem(lane, heads) // (heads // 2)) == lax.rem(s + 1, 2)
+    for which in range(2):
+        kv_t[which, :, tokens:] = kv[which, tokens:].T
+
     diag_key = lax.broadcasted_iota(jnp.int32, (chunk_tok, chunk), 0)
-    diag_tok = lax.broadcasted_iota(jnp.int32, (chunk_tok, chunk), 1) // heads
+    diag_tok = lax.rem(lax.broadcasted_iota(jnp.int32, (chunk_tok, chunk), 1), chunk_tok)
     diag = diag_key <= diag_tok
 
-    for a in range(chunks):
-        here = pl.ds(a * chunk, chunk)
-        own_keys = chunk_tok * (a + 1)
+    def own_tile(part, c):
+        here = slice(c * chunk, (c + 1) * chunk)
+        own_keys = chunk_tok * (c + 1)
         inner = own_keys - chunk_tok
-        scores = dot(kv[0, tokens : tokens + own_keys, :], q_ref[here, :], NT) * unit
+        scores = dot(kv[0, tokens : tokens + own_keys, :], q_ref[part, here, :], NT) * unit
         edge = jnp.where(diag, scores[inner:], -jnp.inf)
         top = jnp.max(edge, axis=0, keepdims=True)
-        if a:
+        if c:
             top = jnp.maximum(top, jnp.max(scores[:inner], axis=0, keepdims=True))
             edge = jnp.concatenate([scores[:inner], edge], axis=0)
         probs = jnp.exp2(edge - top)
-        prob_grad = dot(kv[1, tokens : tokens + own_keys, :], g_ref[here, :], NT)
+        prob_grad = dot(kv[1, tokens : tokens + own_keys, :], g_ref[part, here, :], NT)
+        return top, jnp.sum(probs, axis=0, keepdims=True), probs, prob_grad
+
+    def keep(part, c, weights, score_grad):
+        here = slice(c * chunk, (c + 1) * chunk)
+        top = tokens + chunk_tok * (c + 1)
+        limit = tokens + -(-(chunk_tok * (c + 1)) // 128) * 128
+        w_ref[part, tokens:top, here] = weights.astype(jnp.bfloat16)
+        ds_ref[part, tokens:top, here] = score_grad.astype(jnp.bfloat16)
+        if limit > top:
+            blank = jnp.zeros((limit - top, chunk), jnp.bfloat16)
+            w_ref[part, top:limit, here] = blank
+            ds_ref[part, top:limit, here] = blank
+
+    def own_grad(part, which, low):
+        keys = slice(tokens + low, tokens + low + 128)
+        first = low * half
+        left, right = ((ds_ref, q_ref), (w_ref, g_ref))[which]
+        return dot(left[part, keys, first:], right[part, first:, :])
+
+    def row_outputs(part, c):
+        here = slice(c * chunk, (c + 1) * chunk)
+        low = 0 if part else tokens
+        limit = tokens + -(-(chunk_tok * (c + 1)) // 128) * 128
+        out = dot(kv_t[1, :, low:limit], w_ref[part, low:limit, here])
+        grad = dot(kv_t[0, :, low:limit], ds_ref[part, low:limit, here]) * scale
+        for i, value in enumerate((out, grad)):
+            value = value.astype(jnp.bfloat16).T.astype(jnp.float32)
+            for j in range(half):
+                flat_out[i, head_rows(part, c, j), :] = value[j * chunk_tok : (j + 1) * chunk_tok]
+
+    for c in range(chunks):
+        here = slice(c * chunk, (c + 1) * chunk)
+        own_keys = chunk_tok * (c + 1)
+        top, total, probs, prob_grad = own_tile(1, c)
         p_own[:own_keys, here] = probs
         dp_own[:own_keys, here] = prob_grad
         stats[0:1, here] = top
-        stats[1:2, here] = jnp.sum(probs, axis=0, keepdims=True)
+        stats[1:2, here] = total
         stats[2:3, here] = jnp.sum(probs * prob_grad, axis=0, keepdims=True)
+    for c in range(chunks):
+        _, total, probs, prob_grad = own_tile(0, c)
+        weights = probs * (1.0 / total)
+        delta = jnp.sum(weights * prob_grad, axis=0, keepdims=True)
+        keep(0, c, weights, weights * (prob_grad - delta))
+    for which in range(2):
+        for low in range(0, tokens, 128):
+            own_sum[which, low : low + 128] = own_grad(0, which, low)
+    for c in range(chunks):
+        row_outputs(0, c)
 
     def send_grads(block, which, slot, target, d):
         return pltpu.make_async_remote_copy(
@@ -366,72 +422,57 @@
 
     for copy in prev_copies[0]:
         copy.wait()
-    for a in range(chunks):
-        here = pl.ds(a * chunk, chunk)
-        scores = dot(kv[0, :tokens, :], q_ref[here, :], NT) * unit
+    for c in range(chunks):
+        here = slice(c * chunk, (c + 1) * chunk)
+        scores = dot(kv[0, :tokens, :], q_ref[1, here, :], NT) * unit
         top_own = stats[0:1, here]
-        top = jnp.where(sees_prev, jnp.max(scores, axis=0, keepdims=True), -jnp.inf)
-        top = jnp.maximum(top, top_own)
-        probs = jnp.exp2(scores - jnp.where(sees_prev, top, 1e30))
+        top = jnp.maximum(jnp.max(scores, axis=0, keepdims=True), top_own)
+        probs = jnp.exp2(scores - top)
         factor = jnp.exp2(top_own - top)
         inverse = 1.0 / (jnp.sum(probs, axis=0, keepdims=True) + factor * stats[1:2, here])
-        w_ref[:tokens, here] = (probs * inverse).astype(jnp.bfloat16)
+        w_ref[1, :tokens, here] = (probs * inverse).astype(jnp.bfloat16)
         stats[3:4, here] = factor * inverse
-    g_send[0, 1] = dot(w_ref[:tokens, :], g_ref[...]).astype(jnp.bfloat16)
+    g_send[0, 1] = dot(w_ref[1, :tokens, :], g_ref[1]).astype(jnp.bfloat16)
     prev_v_grads = [send_grads(0, 1, peers + d, before, d) for d in range(peers)]
     for copy in prev_v_grads:
         copy.start()
 
     for copy in prev_copies[1]:
         copy.wait()
-    for a in range(chunks):
-        here = pl.ds(a * chunk, chunk)
-        weights = w_ref[:tokens, here].astype(jnp.float32)
-        prob_grad = dot(kv[1, :tokens, :], g_ref[here, :], NT)
+    for c in range(chunks):
+        here = slice(c * chunk, (c + 1) * chunk)
+        weights = w_ref[1, :tokens, here].astype(jnp.float32)
+        prob_grad = dot(kv[1, :tokens, :], g_ref[1, here, :], NT)
         delta = jnp.sum(weights * prob_grad, axis=0, keepdims=True) + stats[3:4, here] * stats[2:3, here]
         stats[4:5, here] = delta
-        ds_ref[:tokens, here] = (weights * (prob_grad - delta)).astype(jnp.bfloat16)
-    g_send[0, 0] = (dot(ds_ref[:tokens, :], q_ref[...]) * scale).astype(jnp.bfloat16)
+        ds_ref[1, :tokens, here] = (weights * (prob_grad - delta)).astype(jnp.bfloat16)
+    g_send[0, 0] = (dot(ds_ref[1, :tokens, :], q_ref[1]) * scale).astype(jnp.bfloat16)
     prev_k_grads = [send_grads(0, 0, d, before, d) for d in range(peers)]
     for copy in prev_k_grads:
         copy.start()
 
-    for a in range(chunks):
-        here = pl.ds(a * chunk, chunk)
-        own_keys = chunk_tok * (a + 1)
+    for c in range(chunks):
+        here = slice(c * chunk, (c + 1) * chunk)
+        own_keys = chunk_tok * (c + 1)
         weights = p_own[:own_keys, here] * stats[3:4, here]
-        w_ref[tokens : tokens + own_keys, here] = weights.astype(jnp.bfloat16)
-        ds_ref[tokens : tokens + own_keys, here] = (
-            weights * (dp_own[:own_keys, here] - stats[4:5, here])
-        ).astype(jnp.bfloat16)
-        limit = -(-own_keys // 128) * 128
-        if limit > own_keys:
-            blank = jnp.zeros((limit - own_keys, chunk), jnp.bfloat16)
-            w_ref[tokens + own_keys : tokens + limit, here] = blank
-            ds_ref[tokens + own_keys : tokens + limit, here] = blank
-    for low in range(0, tokens, 128):
-        keys = slice(tokens + low, tokens + low + 128)
-        first = low * heads
-        g_send[1, 1, low : low + 128] = dot(w_ref[keys, first:], g_ref[first:, :]).astype(jnp.bfloat16)
-        g_send[1, 0, low : low + 128] = (dot(ds_ref[keys, first:], q_ref[first:, :]) * scale).astype(
-            jnp.bfloat16
-        )
-    own_grads = [
-        send_grads(1, which, (2 + which) * peers + d, s, d)
-        for which in range(2)
-        for d in range(1, peers)
-    ]
-    for copy in own_grads:
-        copy.start()
+        keep(1, c, weights, weights * (dp_own[:own_keys, here] - stats[4:5, here]))
+    own_grads = []
+    for which, factor in ((1, 1.0), (0, scale)):
+        for low in range(0, tokens, 128):
+            total = own_sum[which, low : low + 128] + own_grad(1, which, low)
+            g_send[1, which, low : low + 128] = (total * factor).astype(jnp.bfloat16)
+        copies = [send_grads(1, which, (2 + which) * peers + d, s, d) for d in range(1, peers)]
+        for copy in copies:
+            copy.start()
+        own_grads += copies
     g_land[1, h] = g_send[1, :, mine, :]
 
     for which in range(2):
-        kv_t[which] = kv[which].T
-    for a in range(chunks):
-        here = pl.ds(a * chunk, chunk)
-        limit = tokens + -(-(chunk_tok * (a + 1)) // 128) * 128
-        att_ref[here, :] = dot(kv_t[1, :, :limit], w_ref[:limit, here]).astype(jnp.bfloat16).T
-        dq_ref[here, :] = (dot(kv_t[0, :, :limit], ds_ref[:limit, here]) * scale).astype(jnp.bfloat16).T
+        kv_t[which, :, :tokens] = kv[which, :tokens].T
+    for c in range(chunks):
+        row_outputs(1, c)
+    att_ref[...] = flat_out[0].astype(jnp.bfloat16)
+    dq_ref[...] = flat_out[1].astype(jnp.bfloat16)
 
     for copy in prev_v_grads + prev_k_grads + own_grads:
         copy.wait()
@@ -476,18 +517,21 @@
         in_specs=[hbm] * 4,
         out_specs=(vmem,) * 4,
         scratch_shapes=[
-            pltpu.VMEM((rows, head_dim), bf16),
-            pltpu.VMEM((rows, head_dim), bf16),
+            pltpu.VMEM((rows, head_dim), f32),
+            pltpu.VMEM((2, rows, head_dim), f32),
+            pltpu.VMEM((2, rows // 2, head_dim), bf16),
+            pltpu.VMEM((2, rows // 2, head_dim), bf16),
             pltpu.VMEM((2, kv_rows, head_dim), bf16),
             pltpu.VMEM((2, kv_rows, head_dim), f32),
             pltpu.VMEM((peers, 2, piece, head_dim), bf16),
             pltpu.VMEM((2, 2 * tokens, head_dim), bf16),
             pltpu.VMEM((2, head_dim, 2 * tokens), bf16),
-            pltpu.VMEM((tokens, rows), f32),
-            pltpu.VMEM((tokens, rows), f32),
-            pltpu.VMEM((8, rows), f32),
-            pltpu.VMEM((2 * tokens, rows), bf16),
-            pltpu.VMEM((2 * tokens, rows), bf16),
+            pltpu.VMEM((tokens, rows // 2), f32),
+            pltpu.VMEM((tokens, rows // 2), f32),
+            pltpu.VMEM((8, rows // 2), f32),
+            pltpu.VMEM((2, 2 * tokens, rows // 2), bf16),
+            pltpu.VMEM((2, 2 * tokens, rows // 2), bf16),
+            pltpu.VMEM((2, tokens, head_dim), f32),
             pltpu.VMEM((2, 2, tokens, head_dim), bf16),
             pltpu.VMEM((2, peers, 2, piece, head_dim), bf16),
             dma((4,)),

time: 20.6 us -> 19.1 us (0.927)
  Pallas kernels: 19.8 us -> 18.3 us
    pallas_call x1, Pallas kernels: 18.8 us -> 17.3 us  [fused_device(): pl.pallas_call(functools.partial(fused_kernel, devices, peers, heads), ou...]
where the time goes in v3:
time: 19.1 us; the launch traced here: 18.9 us
  Pallas kernels  18.3 us (96%)
  between operations  0.64 us (3%)
    pallas_call x1, Pallas kernels, fused_device(): pl.pallas_call(functools.partial(fused_kernel, devices, peers, heads), ou...  17.3 us
    pallas_call x1, Pallas kernels, fused_device(): pl.pallas_call(place_kernel, out_shape=(big, big, small, small), in_specs...  1.03 us

profile of v3, /device:TPU:0, one launch (start us, length us, event | category | flops | bytes accessed | tf_op | source)
XLA Modules:
  0.0 18.9 jit_solution(12804598811149546033)
XLA Ops:
  0.6 17.3 %shard_map.75 = (bf16[2048,128]{1,0:T(8,128)(2,1)S(1)}, bf16[2048,128]{1,0:T(8,128)(2,1)S(1)}, bf16[256,128]{1,0:T(8,128)(2,1)S(1)}, bf16[256,128]{1,0:T(8,128)(2,1)S(1)}) custom-call(bf16[2048,128]{1,0:T(8,128)(2,1)} %bitcast.8, bf16[256,128]{1,0:T(8,128)(2,1)} %bitcast.10, bf16[256,128]{1,0:T(8,128)(2,1)} %bitcast.11, bf16[2048,128]{1,0:T(8,128)(2,1)} %bitcast.9), custom_call_target="tpu_custom_call" | custom-call | tf_op jit(solution)/shard_map/pallas_call | solution.py:514
  17.9 1.0 %shard_map.76 = (bf16[2048,128]{1,0:T(8,128)(2,1)}, bf16[2048,128]{1,0:T(8,128)(2,1)}, bf16[256,128]{1,0:T(8,128)(2,1)}, bf16[256,128]{1,0:T(8,128)(2,1)}) custom-call(bf16[2048,128]{1,0:T(8,128)(2,1)S(1)} %get-tuple-element.12.refs_0_, bf16[2048,128]{1,0:T(8,128)(2,1)S(1)} %get-tuple-element.13.refs_1_, bf16[256,128]{1,0:T(8,128)(2,1)S(1)} %get-tuple-element.14.refs_2_, ...), custom_call_target="tpu_custom_call" | custom-call | tf_op jit(solution)/shard_map/pallas_call | solution.py:552

commit v4 on v3

--- a/solution.py
+++ b/solution.py
@@ -213,8 +213,16 @@
 
 
 def pair_groups(devices, head_devices, sizes):
-    _, kv_rows, kv_heads, head_dim = sizes
-    return devices == 2 * GROUPS and kv_heads == head_devices and head_dim == 128
+    tokens, heads, kv_heads, head_dim = sizes
+    local = tokens // devices
+    return (
+        devices == 2 * GROUPS
+        and kv_heads == head_devices
+        and heads == 8 * kv_heads
+        and head_devices % 2 == 0
+        and head_dim == 128
+        and local % 256 == 0
+    )
 
 
 NT = (((1,), (1,)), ((), ()))
@@ -276,7 +284,9 @@
     bases = (lax.rem(s, 2) * half, lax.rem(s + 1, 2) * half)
 
     def peer(d):
-        return lax.rem(h + d, peers)
+        return lax.rem(h // 2 + d // 2, peers // 2) * 2 + lax.rem(h + d, 2)
+
+    far_first = [*range(2, peers), *range(2)]
 
     raw = ((k_hbm, kv_in.at[0]), (v_hbm, kv_in.at[1]), (q_hbm, att_ref), (g_hbm, dq_ref))
     loads = [pltpu.make_async_copy(src, dst, load_sem.at[i]) for i, (src, dst) in enumerate(raw)]
@@ -310,14 +320,14 @@
         )
 
     own_copies = [
-        send_kv(d, kv_send.at[peer(d)], kv.at[:, mine_own, :], s, d) for d in range(1, peers)
+        send_kv(d, kv_send.at[peer(d)], kv.at[:, mine_own, :], s, d) for d in far_first if d
     ]
     prev_copies = [
         [
             send_kv(
                 (1 + which) * peers + d, kv_send.at[peer(d), which], kv.at[which, mine, :], after, d
             )
-            for d in range(peers)
+            for d in far_first
         ]
         for which in range(2)
     ]
@@ -433,7 +443,7 @@
         w_ref[1, :tokens, here] = (probs * inverse).astype(jnp.bfloat16)
         stats[3:4, here] = factor * inverse
     g_send[0, 1] = dot(w_ref[1, :tokens, :], g_ref[1]).astype(jnp.bfloat16)
-    prev_v_grads = [send_grads(0, 1, peers + d, before, d) for d in range(peers)]
+    prev_v_grads = [send_grads(0, 1, peers + d, before, d) for d in far_first]
     for copy in prev_v_grads:
         copy.start()
 
@@ -447,7 +457,7 @@
         stats[4:5, here] = delta
         ds_ref[1, :tokens, here] = (weights * (prob_grad - delta)).astype(jnp.bfloat16)
     g_send[0, 0] = (dot(ds_ref[1, :tokens, :], q_ref[1]) * scale).astype(jnp.bfloat16)
-    prev_k_grads = [send_grads(0, 0, d, before, d) for d in range(peers)]
+    prev_k_grads = [send_grads(0, 0, d, before, d) for d in far_first]
     for copy in prev_k_grads:
         copy.start()
 
@@ -461,7 +471,7 @@
         for low in range(0, tokens, 128):
             total = own_sum[which, low : low + 128] + own_grad(1, which, low)
             g_send[1, which, low : low + 128] = (total * factor).astype(jnp.bfloat16)
-        copies = [send_grads(1, which, (2 + which) * peers + d, s, d) for d in range(1, peers)]
+        copies = [send_grads(1, which, (2 + which) * peers + d, s, d) for d in far_first if d]
         for copy in copies:
             copy.start()
         own_grads += copies

time: 19.1 us -> 18.8 us (0.984)
  Pallas kernels: 18.3 us -> 18 us
    pallas_call x1, Pallas kernels: 17.3 us -> 17 us  [fused_device(): pl.pallas_call(functools.partial(fused_kernel, devices, peers, heads), ou...]
where the time goes in v4:
time: 18.8 us; the launch traced here: 18.6 us
  Pallas kernels  18 us (96%)
  between operations  0.64 us (3%)
    pallas_call x1, Pallas kernels, fused_device(): pl.pallas_call(functools.partial(fused_kernel, devices, peers, heads), ou...  17 us
    pallas_call x1, Pallas kernels, fused_device(): pl.pallas_call(place_kernel, out_shape=(big, big, small, small), in_specs...  1.03 us

profile of v4, /device:TPU:0, one launch (start us, length us, event | category | flops | bytes accessed | tf_op | source)
XLA Modules:
  0.0 18.6 jit_solution(2352027462857291739)
XLA Ops:
  0.6 17.0 %shard_map.75 = (bf16[2048,128]{1,0:T(8,128)(2,1)S(1)}, bf16[2048,128]{1,0:T(8,128)(2,1)S(1)}, bf16[256,128]{1,0:T(8,128)(2,1)S(1)}, bf16[256,128]{1,0:T(8,128)(2,1)S(1)}) custom-call(bf16[2048,128]{1,0:T(8,128)(2,1)} %bitcast.8, bf16[256,128]{1,0:T(8,128)(2,1)} %bitcast.10, bf16[256,128]{1,0:T(8,128)(2,1)} %bitcast.11, bf16[2048,128]{1,0:T(8,128)(2,1)} %bitcast.9), custom_call_target="tpu_custom_call" | custom-call | tf_op jit(solution)/shard_map/pallas_call | solution.py:524
  17.6 1.0 %shard_map.76 = (bf16[2048,128]{1,0:T(8,128)(2,1)}, bf16[2048,128]{1,0:T(8,128)(2,1)}, bf16[256,128]{1,0:T(8,128)(2,1)}, bf16[256,128]{1,0:T(8,128)(2,1)}) custom-call(bf16[2048,128]{1,0:T(8,128)(2,1)S(1)} %get-tuple-element.12.refs_0_, bf16[2048,128]{1,0:T(8,128)(2,1)S(1)} %get-tuple-element.13.refs_1_, bf16[256,128]{1,0:T(8,128)(2,1)S(1)} %get-tuple-element.14.refs_2_, ...), custom_call_target="tpu_custom_call" | custom-call | tf_op jit(solution)/shard_map/pallas_call | solution.py:562

commit v5 on v4

--- a/solution.py
+++ b/solution.py
@@ -485,13 +485,15 @@
     dq_ref[...] = flat_out[1].astype(jnp.bfloat16)
 
     for copy in prev_v_grads + prev_k_grads + own_grads:
-        copy.wait()
+        copy.wait_recv()
     for which, out in ((0, dk_ref), (1, dv_ref)):
         for p in range(peers):
             spread[which, pl.ds(p, piece, stride=peers), :] = g_land[0, p, which].astype(
                 jnp.float32
             ) + g_land[1, p, which].astype(jnp.float32)
         out[...] = spread[which].astype(jnp.bfloat16)
+    for copy in prev_v_grads + prev_k_grads + own_grads:
+        copy.wait_send()
 
 
 def place_kernel(*refs):

time: 18.8 us -> 18.8 us (level)
  no operation moved by 1% of the time
where the time goes in v5:
time: 18.8 us; the launch traced here: 18.7 us
  Pallas kernels  18 us (96%)
  between operations  0.64 us (3%)
    pallas_call x1, Pallas kernels, fused_device(): pl.pallas_call(functools.partial(fused_kernel, devices, peers, heads), ou...  17 us
    pallas_call x1, Pallas kernels, fused_device(): pl.pallas_call(place_kernel, out_shape=(big, big, small, small), in_specs...  1.03 us

profile of v5, /device:TPU:0, one launch (start us, length us, event | category | flops | bytes accessed | tf_op | source)
XLA Modules:
  0.0 18.7 jit_solution(3251092544656880123)
XLA Ops:
  0.6 17.0 %shard_map.75 = (bf16[2048,128]{1,0:T(8,128)(2,1)S(1)}, bf16[2048,128]{1,0:T(8,128)(2,1)S(1)}, bf16[256,128]{1,0:T(8,128)(2,1)S(1)}, bf16[256,128]{1,0:T(8,128)(2,1)S(1)}) custom-call(bf16[2048,128]{1,0:T(8,128)(2,1)} %bitcast.8, bf16[256,128]{1,0:T(8,128)(2,1)} %bitcast.10, bf16[256,128]{1,0:T(8,128)(2,1)} %bitcast.11, bf16[2048,128]{1,0:T(8,128)(2,1)} %bitcast.9), custom_call_target="tpu_custom_call" | custom-call | tf_op jit(solution)/shard_map/pallas_call | solution.py:526
  17.6 1.0 %shard_map.76 = (bf16[2048,128]{1,0:T(8,128)(2,1)}, bf16[2048,128]{1,0:T(8,128)(2,1)}, bf16[256,128]{1,0:T(8,128)(2,1)}, bf16[256,128]{1,0:T(8,128)(2,1)}) custom-call(bf16[2048,128]{1,0:T(8,128)(2,1)S(1)} %get-tuple-element.12.refs_0_, bf16[2048,128]{1,0:T(8,128)(2,1)S(1)} %get-tuple-element.13.refs_1_, bf16[256,128]{1,0:T(8,128)(2,1)S(1)} %get-tuple-element.14.refs_2_, ...), custom_call_target="tpu_custom_call" | custom-call | tf_op jit(solution)/shard_map/pallas_call | solution.py:564
